TPU v7x, 32 devices: a whole 2x2x4 slice. The times are simulated.
32 devices in a mesh: groups: 2 (over x), tensor: 16 (over z, y, core).
Axes of the slice: x: 2, y: 2, z: 4, core: 2. Of those that a mesh axis runs over, the one named last changes fastest.
Arguments:
- residual_in: bfloat16 [1024, 6144], P('groups', 'tensor'), parts along dimension 0
- norm_gain: bfloat16 [6144], P('tensor'), may hold values from 0.099609375 to 1.8984375
- final_gain: bfloat16 [6144], P('tensor'), may hold values from 0.099609375 to 1.8984375
- expert_ids: int32 [1024, 2], P('groups'), parts along dimension 0, may hold values from 0 to 3, all different within a row; in each aligned block of 512 rows (0 to 511, 512 to 1023, ...) at most 384 rows name the same one
- gate_values: float32 [1024, 2], P('groups'), parts along dimension 0, may hold values from 0.2 to 1
- w_gate: bfloat16 [6144, 32768], P(None, 'tensor'), may hold values from -0.078125 to 0.078125
- w_up: bfloat16 [6144, 32768], P(None, 'tensor'), may hold values from -0.078125 to 0.078125
- w_down: bfloat16 [32768, 6144], P('tensor')
- lm_head: bfloat16 [6144, 32768], P(None, 'tensor')
- target_ids: int32 [1024], P('groups'), parts along dimension 0, may hold values from 0 to 32767
- lengths: int32 [16], P('groups'), parts along dimension 0, may hold values from 1 to 64
Outputs:
- masked_logprob: float32 [1024], P(('groups', 'tensor')), parts along dimension 0
There are 2 independent parts, one for each index of `groups`. A program takes and returns all parts, laid end to end along the dimension named above; an argument that names none is the same for every part. Nothing has to cross between parts.
Inputs may be any that keep to these rules, and one draw needn't show every extreme that they name: `expert_ids`: no expert is named by more than 384 tokens of a frontier batch, a bound that some block reaches.
All inputs are finite; a program needn't handle non-finite values.
Results may differ from a plain program's by a relative error of at most 0.0055.
Values may be sent and summed in bfloat16 or wider, within the bound.
No kernel may reach another device: no remote copies, remote signals or barrier semaphores. Data moves between devices by JAX's collectives and lax.ppermute only.
A program may use at most 192 MiB of HBM per device.

v0:
```python
import jax
import jax.numpy as jnp
from jax import lax
from jax.sharding import PartitionSpec as P

D = 6144
EXPERTS = 4
EXP_FF = 8192
TOP = 2
SEQ = 64
CAP = 384


epsilon = 1e-05


def combined_all(array, axis, combine):
    everything = jax.tree.map(lambda part: lax.all_gather(part, axis), array)
    leading = jax.tree.map(lambda part: part[0], everything)

    def hop(k, so_far):
        return combine(so_far, jax.tree.map(lambda part: part[k], everything))

    return lax.fori_loop(1, lax.axis_size(axis), hop, leading)


def slots_of(expert_ids):
    flat_ids = expert_ids.reshape(-1)
    one_hot = (flat_ids[:, None] == jnp.arange(EXPERTS, dtype=jnp.int32)[None, :]).astype(jnp.int32)
    earlier = jnp.cumsum(one_hot, axis=0) - one_hot
    return jnp.sum(earlier * one_hot, axis=1).reshape(expert_ids.shape)


def slot_tokens(expert_ids, slot_index):
    slot_code = (expert_ids * CAP + slot_index).reshape(-1)
    owner = jnp.arange(slot_code.shape[0], dtype=jnp.int32) // TOP
    wanted = jnp.arange(EXPERTS * CAP, dtype=jnp.int32)
    matches = slot_code[None, :] == wanted[:, None]
    return jnp.sum(jnp.where(matches, owner[None, :] + 1, 0), axis=1) - 1


def normalize(values, squares_total, gain_vec):
    return (
        values / jnp.sqrt(squares_total[:, None] / D + epsilon) * gain_vec.astype(jnp.float32)
    ).astype(jnp.bfloat16)


def body(
    residual_in,
    norm_gain,
    final_gain,
    expert_ids,
    gate_values,
    w_gate,
    w_up,
    w_down,
    lm_head,
    target_ids,
    lengths,
):
    tokens, feature_cols = residual_in.shape
    hidden_dev = w_gate.shape[1]
    per_expert = EXP_FF // hidden_dev
    expert_now = lax.axis_index("tensor") // per_expert
    stream = residual_in.astype(jnp.float32)
    in_total = lax.psum(jnp.sum(stream * stream, axis=1), "tensor")
    normed = normalize(stream, in_total, norm_gain)
    slot_index = slots_of(expert_ids)
    token_of = slot_tokens(expert_ids, slot_index)
    zero_bf = jnp.zeros((), jnp.bfloat16)
    own_slots = lax.dynamic_slice_in_dim(token_of, expert_now * CAP, CAP)
    occupied = own_slots >= 0
    safe_index = jnp.maximum(own_slots, 0)
    slot_rows = jnp.where(
        occupied[:, None], lax.all_gather(normed, "tensor", axis=1, tiled=True)[safe_index], zero_bf
    )
    gate_out = jnp.dot(slot_rows, w_gate, preferred_element_type=jnp.float32)
    up_out = jnp.dot(slot_rows, w_up, preferred_element_type=jnp.float32)
    hidden = (jax.nn.silu(gate_out) * up_out).astype(jnp.bfloat16)
    partial_value = jnp.dot(hidden, w_down, preferred_element_type=jnp.float32)
    weight_own = jnp.where(expert_ids == expert_now, gate_values, jnp.zeros_like(gate_values))
    weighted = (
        weight_own[:, 0:1] * partial_value[slot_index[:, 0]]
        + weight_own[:, 1:2] * partial_value[slot_index[:, 1]]
    )
    moe_cols = lax.psum_scatter(weighted, "tensor", scatter_dimension=1, tiled=True)
    mixture = stream + moe_cols
    out_total = lax.psum(jnp.sum(mixture * mixture, axis=1), "tensor")
    normed_out = normalize(mixture, out_total, final_gain)
    vocab_dev = lm_head.shape[1]
    logits = jnp.dot(
        lax.all_gather(normed_out, "tensor", axis=1, tiled=True),
        lm_head,
        preferred_element_type=jnp.float32,
    )
    row_max = jnp.max(logits, axis=1)
    row_total = jnp.sum(jnp.exp(logits - row_max[:, None]), axis=1)
    local_ids = target_ids - lax.axis_index("tensor") * vocab_dev
    vocab_cols = jnp.arange(vocab_dev, dtype=jnp.int32)
    picked = jnp.sum(jnp.where(vocab_cols[None, :] == local_ids[:, None], logits, 0.0), axis=1)

    def joined(earlier, later):
        merged_max = jnp.maximum(earlier[0], later[0])
        merged_total = earlier[1] * jnp.exp(earlier[0] - merged_max) + later[1] * jnp.exp(
            later[0] - merged_max
        )
        return (merged_max, merged_total, earlier[2] + later[2])

    merged_max, merged_total, target_logit = combined_all(
        (row_max, row_total, picked), "tensor", joined
    )
    logprob = target_logit - merged_max - jnp.log(merged_total)
    rows_dev = tokens // lax.axis_size("tensor")
    first_row = lax.axis_index("tensor") * rows_dev
    own_rows = lax.dynamic_slice_in_dim(logprob, first_row, rows_dev)
    position = first_row + jnp.arange(rows_dev, dtype=jnp.int32)
    in_length = position % SEQ < lengths[position // SEQ]
    return jnp.where(in_length, own_rows, jnp.zeros_like(own_rows)).astype(jnp.float32)


def solution(mesh):
    return jax.shard_map(
        body,
        mesh=mesh,
        in_specs=(
            P("groups", "tensor"),
            P("tensor"),
            P("tensor"),
            P("groups", None),
            P("groups", None),
            P(None, "tensor"),
            P(None, "tensor"),
            P("tensor", None),
            P(None, "tensor"),
            P("groups"),
            P("groups"),
        ),
        out_specs=P(("groups", "tensor")),
        check_vma=False,
    )
```

profile of v0, /device:TPU:0, one launch (start us, length us, event | category | flops | bytes accessed | tf_op | source)
XLA Modules:
  0.0 533.9 jit_solution(7636073680571845794)
XLA Ops:
  6.5 1.2 fusion.3
  7.7 34.9 %psum.14 = f32[512]{0:T(512)S(1)} all-reduce(f32[512]{0:T(512)S(1)} %fusion.3), channel_id=1, replica_groups=mesh['groups'=2,'tensor'=16] {'tensor'}, use_global_device_ids=true, to_apply=%region_5.6 | all-reduce | flops 512 | bytes 4096 | tf_op jit(solution)/shard_map/psum | solution.py:66
  42.6 0.7 convert_element_type.28
  43.3 1.9 fusion.5
  45.3 0.8 copy.28
  46.5 1.1 reduce-window.6
  48.5 0.7 multiply_add_fusion.2
  49.6 0.7 select_reduce_fusion
  50.5 0.3 fusion.6
  50.8 0.7 compare_select_fusion.2
  51.5 56.9 %all-gather.9.cloned.1.call-done = bf16[512,6144]{1,0:T(8,128)(2,1)} async-done(((bf16[512,384]{1,0:T(8,128)(2,1)}), bf16[512,6144]{1,0:T(8,128)(2,1)}) %all-gather.9.cloned.1.call-update) | async-done | bytes 6291472 | tf_op jit(solution)/shard_map/all_gather | solution.py:75
  108.4 15.3 %gather_fusion.1 = bf16[384,6144]{1,0:T(8,128)(2,1)} fusion(bf16[512,6144]{1,0:T(8,128)(2,1)} %all-gather.9.cloned.1.call-done, s32[1024]{0:T(1024)S(1)} %pad_clamp_fusion.2), kind=kCustom, calls=%fused_computation.1 | custom fusion | bytes 9438720 | tf_op jit(solution)/shard_map/gather | solution.py:75
  123.7 16.5 %fusion.1 = f32[384,2048]{1,0:T(8,128)S(1)} fusion(bf16[6144,2048]{1,0:T(8,128)(2,1)} %param.18, bf16[384,6144]{1,0:T(8,128)(2,1)} %gather_fusion.1, pred[384]{0:T(512)(128)(4,1)S(1)} %fusion.16), kind=kOutput, calls=%fused_computation.17 | convolution fusion | flops 9666035712 | bytes 33030528 | tf_op jit(solution)/shard_map/dot_general | solution.py:77
  140.2 15.4 %multiply_convert_fusion.clone.4 = bf16[384,2048]{1,0:T(8,128)(2,1)S(1)} fusion(f32[384,2048]{1,0:T(8,128)S(1)} %fusion.1, bf16[6144,2048]{1,0:T(8,128)(2,1)} %param.19, bf16[384,6144]{1,0:T(8,128)(2,1)S(1)} %copy-done.2, pred[384]{0:T(512)(128)(4,1)S(1)} %fusion.16), kind=kOutput, calls=%fused_computation.15.clone.clone.clone.1 | convolution fusion | flops 9670754304 | bytes 34603392 | tf_op jit(solution)/shard_map/dot_general | solution.py:78
  155.6 17.0 %fusion = f32[384,6144]{1,0:T(8,128)} fusion(bf16[2048,6144]{1,0:T(8,128)(2,1)} %param.20, bf16[384,2048]{1,0:T(8,128)(2,1)S(1)} %multiply_convert_fusion.clone.4), kind=kOutput, calls=%fused_computation.16 | convolution fusion | flops 9663676416 | bytes 36175872 | tf_op jit(solution)/shard_map/dot_general | solution.py:80
  172.6 16.3 %gather_fusion.2 = f32[512,6144]{1,0:T(8,128)} fusion(f32[384,6144]{1,0:T(8,128)} %fusion, s32[1024]{0:T(1024)S(1)} %get-tuple-element.213), kind=kCustom, calls=%fused_computation.2 | custom fusion | bytes 25167872 | tf_op jit(solution)/shard_map/gather | solution.py:83
  188.8 16.2 %gather_fusion.3 = f32[512,6144]{1,0:T(8,128)} fusion(f32[384,6144]{1,0:T(8,128)} %fusion, s32[1024]{0:T(1024)S(1)} %get-tuple-element.212), kind=kCustom, calls=%fused_computation.3 | custom fusion | bytes 25167872 | tf_op jit(solution)/shard_map/gather | solution.py:84
  205.0 14.0 %multiply_add_fusion.1 = f32[512,6144]{1,0:T(8,128)} fusion(f32[512,6144]{1,0:T(8,128)} %gather_fusion.3, f32[512,6144]{1,0:T(8,128)} %gather_fusion.2, f32[512]{0:T(512)S(1)} %bitcast.70, f32[512]{0:T(512)S(1)} %bitcast.69), kind=kLoop, calls=%fused_computation.8 | loop fusion | flops 9437184 | bytes 37752832 | tf_op jit(solution)/shard_map/add | solution.py:83
  219.1 0.6 copy-done.4
  219.7 132.4 %reduce-scatter.2.cloned.1.call-done = f32[512,384]{1,0:T(8,128)} async-done(((f32[512,6144]{1,0:T(8,128)}), f32[512,384]{1,0:T(8,128)}) %reduce-scatter.2.cloned.1.call-update) | async-done | bytes 786448 | tf_op jit(solution)/shard_map/reduce_scatter | solution.py:86
  352.1 1.3 multiply_reduce_fusion
  353.4 31.6 %psum.15 = f32[512]{0:T(512)S(1)} all-reduce(f32[512]{0:T(512)S(1)} %multiply_reduce_fusion), channel_id=1, replica_groups=mesh['groups'=2,'tensor'=16] {'tensor'}, use_global_device_ids=true, to_apply=%region_8.9 | all-reduce | flops 512 | bytes 4096 | tf_op jit(solution)/shard_map/psum | solution.py:88
  385.0 2.1 multiply_convert_fusion.1
  387.2 0.7 gather_fusion
  387.9 62.3 %all-gather.11.cloned.1.call-done = bf16[512,6144]{1,0:T(8,128)(2,1)} async-done(((bf16[512,384]{1,0:T(8,128)(2,1)}), bf16[512,6144]{1,0:T(8,128)(2,1)}) %all-gather.11.cloned.1.call-update) | async-done | bytes 6291472 | tf_op jit(solution)/shard_map/all_gather | solution.py:92
  450.2 18.6 %fusion.25 = (f32[512]{0:T(512)S(1)}, f32[512,2048]{1,0:T(8,128)S(1)}) fusion(bf16[512,6144]{1,0:T(8,128)(2,1)} %all-gather.11.cloned.1.call-done, bf16[6144,2048]{1,0:T(8,128)(2,1)} %param.21), kind=kOutput, calls=%fused_computation.79 | convolution fusion | flops 12885950464 | bytes 35653632 | tf_op jit(solution)/shard_map/dot_general | solution.py:91
  468.8 1.4 select_reduce_fusion.1
  470.2 18.8 %all-gather.4 = f32[16,1,512]{2,1,0:T(1,128)S(1)} all-gather(f32[1,1,512]{2,1,0:T(1,128)S(1)} %bitcast.68), channel_id=3, replica_groups=mesh['groups'=2,'tensor'=16] {'tensor'}, dimensions={0}, use_global_device_ids=true | all-gather | bytes 34816 | tf_op jit(solution)/shard_map/all_gather | solution.py:18
  489.0 17.5 %all-gather.5 = f32[16,1,512]{2,1,0:T(1,128)S(1)} all-gather(f32[1,1,512]{2,1,0:T(1,128)S(1)} %bitcast.67), channel_id=4, replica_groups=mesh['groups'=2,'tensor'=16] {'tensor'}, dimensions={0}, use_global_device_ids=true | all-gather | bytes 34816 | tf_op jit(solution)/shard_map/all_gather | solution.py:18
  506.6 18.8 %all-gather.3 = f32[16,1,512]{2,1,0:T(1,128)S(1)} all-gather(f32[1,1,512]{2,1,0:T(1,128)S(1)} %bitcast.66), channel_id=2, replica_groups=mesh['groups'=2,'tensor'=16] {'tensor'}, dimensions={0}, use_global_device_ids=true | all-gather | bytes 34816 | tf_op jit(solution)/shard_map/all_gather | solution.py:18
  525.4 1.4 while.19
  526.8 0.6 compare_select_fusion.6
  (105 shorter events, 2.7 us)
Async XLA Ops:
  6.5 380.6 %copy-start = (s32[8]{0:T(128)S(1)}, s32[8]{0:T(128)}, u32[]{:S(2)}) copy-start(s32[8]{0:T(128)} %param.23) | copy-start | bytes 100
  6.5 101.8 %all-gather.9.cloned.1.call-start = ((), (), s32[]{:S(2)}) async-start(), calls=%async_computation.1 | async-start | bytes 6684672 | tf_op jit(solution)/shard_map/all_gather | solution.py:75
  45.3 306.8 %reduce-scatter.2.cloned.1.call-start = ((), (), s32[]{:S(2)}) async-start(), calls=%async_computation.2 | async-start | bytes 13369344 | tf_op jit(solution)/shard_map/reduce_scatter | solution.py:86
  123.7 16.5 %copy-start.2 = (bf16[384,6144]{1,0:T(8,128)(2,1)S(1)}, bf16[384,6144]{1,0:T(8,128)(2,1)}, u32[]{:S(2)}) copy-start(bf16[384,6144]{1,0:T(8,128)(2,1)} %gather_fusion.1) | copy-start | bytes 14155780
  219.0 0.7 copy-start.4
  219.0 133.1 %copy-start.1 = (bf16[512,384]{1,0:T(8,128)(2,1)S(1)}, bf16[512,384]{1,0:T(8,128)(2,1)}, u32[]{:S(2)}) copy-start(bf16[512,384]{1,0:T(8,128)(2,1)} %param.13) | copy-start | bytes 1179652
  219.0 168.9 %copy-start.3 = (s32[512]{0:T(512)S(1)}, s32[512]{0:T(512)}, u32[]{:S(2)}) copy-start(s32[512]{0:T(512)} %param.22) | copy-start | bytes 6148
  219.0 231.2 %all-gather.11.cloned.1.call-start = ((), (), s32[]{:S(2)}) async-start(), calls=%async_computation.3 | async-start | bytes 6684672 | tf_op jit(solution)/shard_map/all_gather | solution.py:92
Sparse Core Ops, SparseCore 0:
  45.4 62.9 all-gather.8
  219.1 132.9 reduce-scatter.1
  387.2 62.9 all-gather.10
where the time goes:
time: 535 us; the launch traced here: 534 us
  waiting for transfers between devices  252 us (47%)
  blocking collectives  122 us (23%)
  matrix products  67.5 us (13%)
  local copies, waits for them, and re-layouts  51.4 us (10%)
  other arithmetic  27.7 us (5%)
  between operations  13.3 us (2%)
    reduce_scatter x1, waiting for transfers between devices, body(): lax.psum_scatter(weighted, 'tensor', scatter_dimension=1, tiled=True)  132 us
    all_gather x1, waiting for transfers between devices, body(): lax.all_gather(normed_out, 'tensor', axis=1, tiled=True)  62.3 us
    all_gather x1, waiting for transfers between devices, body(): lax.all_gather(normed, 'tensor', axis=1, tiled=True)[safe_index]  56.9 us
    all_gather x3, blocking collectives, combined_all(): everything = jax.tree.map(lambda part: lax.all_gather(part, axis), array)  55.2 us
    psum x1, blocking collectives, body(): in_total = lax.psum(jnp.sum(stream * stream, axis=1), 'tensor')  34.9 us
    psum x1, blocking collectives, body(): out_total = lax.psum(jnp.sum(mixture * mixture, axis=1), 'tensor')  31.6 us
    dot_general x1, matrix products, body(): jnp.dot(lax.all_gather(normed_out, 'tensor', axis=1, tiled=True), lm_head...  18.6 us
    dot_general x1, matrix products, body(): partial_value = jnp.dot(hidden, w_down, preferred_element_type=jnp.float32)  17 us
  transfers between devices with their start and end apart: 3, of which 3 were waited for; matrix products, arithmetic and copies ran while one was open for 1% of the time, Pallas kernels for 0%

commit v1 on v0

--- a/solution.py
+++ b/solution.py
@@ -26,9 +26,9 @@
 
 def slots_of(expert_ids):
     flat_ids = expert_ids.reshape(-1)
-    one_hot = (flat_ids[:, None] == jnp.arange(EXPERTS, dtype=jnp.int32)[None, :]).astype(jnp.int32)
-    earlier = jnp.cumsum(one_hot, axis=0) - one_hot
-    return jnp.sum(earlier * one_hot, axis=1).reshape(expert_ids.shape)
+    pairs = jnp.arange(flat_ids.shape[0], dtype=jnp.int32)
+    before = (pairs[None, :] < pairs[:, None]) & (flat_ids[None, :] == flat_ids[:, None])
+    return jnp.sum(before.astype(jnp.int32), axis=1).reshape(expert_ids.shape)
 
 
 def slot_tokens(expert_ids, slot_index):

time: 535 us -> 535 us (level)
  no operation moved by 1% of the time
where the time goes in v1:
time: 535 us; the launch traced here: 534 us
  waiting for transfers between devices  253 us (47%)
  blocking collectives  122 us (23%)
  matrix products  67.5 us (13%)
  local copies, waits for them, and re-layouts  51.2 us (10%)
  other arithmetic  26.8 us (5%)
  between operations  13.3 us (2%)
    reduce_scatter x1, waiting for transfers between devices, body(): lax.psum_scatter(weighted, 'tensor', scatter_dimension=1, tiled=True)  132 us
    all_gather x1, waiting for transfers between devices, body(): lax.all_gather(normed_out, 'tensor', axis=1, tiled=True)  62.3 us
    all_gather x1, waiting for transfers between devices, body(): lax.all_gather(normed, 'tensor', axis=1, tiled=True)[safe_index]  58.2 us
    all_gather x3, blocking collectives, combined_all(): everything = jax.tree.map(lambda part: lax.all_gather(part, axis), array)  55.2 us
    psum x1, blocking collectives, body(): in_total = lax.psum(jnp.sum(stream * stream, axis=1), 'tensor')  34.9 us
    psum x1, blocking collectives, body(): out_total = lax.psum(jnp.sum(mixture * mixture, axis=1), 'tensor')  31.6 us
    dot_general x1, matrix products, body(): jnp.dot(lax.all_gather(normed_out, 'tensor', axis=1, tiled=True), lm_head...  18.6 us
    dot_general x1, matrix products, body(): partial_value = jnp.dot(hidden, w_down, preferred_element_type=jnp.float32)  17.2 us
  transfers between devices with their start and end apart: 3, of which 3 were waited for; matrix products, arithmetic and copies ran while one was open for 1% of the time, Pallas kernels for 0%

profile of v1, /device:TPU:0, one launch (start us, length us, event | category | flops | bytes accessed | tf_op | source)
XLA Modules:
  0.0 534.1 jit_solution(18296530312608750279)
XLA Ops:
  6.5 1.2 fusion.4
  7.7 34.9 %psum.14 = f32[512]{0:T(512)S(1)} all-reduce(f32[512]{0:T(512)S(1)} %fusion.4), channel_id=1, replica_groups=mesh['groups'=2,'tensor'=16] {'tensor'}, use_global_device_ids=true, to_apply=%region_3.4 | all-reduce | flops 512 | bytes 4096 | tf_op jit(solution)/shard_map/psum | solution.py:66
  42.6 0.7 convert_element_type.23
  43.3 1.9 fusion.6
  45.4 0.8 copy.24
  46.4 0.5 convert_reduce_fusion
  47.2 0.7 multiply_add_fusion.2
  48.3 0.7 select_reduce_fusion
  49.1 0.3 fusion.7
  49.5 0.7 compare_select_fusion.2
  50.2 58.2 %all-gather.9.cloned.1.call-done = bf16[512,6144]{1,0:T(8,128)(2,1)} async-done(((bf16[512,384]{1,0:T(8,128)(2,1)}), bf16[512,6144]{1,0:T(8,128)(2,1)}) %all-gather.9.cloned.1.call-update) | async-done | bytes 6291472 | tf_op jit(solution)/shard_map/all_gather | solution.py:75
  108.4 15.5 %gather_fusion.1 = bf16[384,6144]{1,0:T(8,128)(2,1)} fusion(bf16[512,6144]{1,0:T(8,128)(2,1)} %all-gather.9.cloned.1.call-done, s32[1024]{0:T(1024)S(1)} %pad_clamp_fusion.2), kind=kCustom, calls=%fused_computation.1 | custom fusion | bytes 9438720 | tf_op jit(solution)/shard_map/gather | solution.py:75
  123.9 16.5 %fusion.2 = f32[384,2048]{1,0:T(8,128)S(1)} fusion(bf16[6144,2048]{1,0:T(8,128)(2,1)} %param.18, bf16[384,6144]{1,0:T(8,128)(2,1)} %gather_fusion.1, pred[384]{0:T(512)(128)(4,1)S(1)} %fusion.13), kind=kOutput, calls=%fused_computation.20 | convolution fusion | flops 9666035712 | bytes 33030528 | tf_op jit(solution)/shard_map/dot_general | solution.py:77
  140.4 15.2 %multiply_convert_fusion.clone.4 = bf16[384,2048]{1,0:T(8,128)(2,1)S(1)} fusion(f32[384,2048]{1,0:T(8,128)S(1)} %fusion.2, bf16[6144,2048]{1,0:T(8,128)(2,1)} %param.19, bf16[384,6144]{1,0:T(8,128)(2,1)S(1)} %copy-done.2, pred[384]{0:T(512)(128)(4,1)S(1)} %fusion.13), kind=kOutput, calls=%fused_computation.18.clone.clone.clone.1 | convolution fusion | flops 9670754304 | bytes 34603392 | tf_op jit(solution)/shard_map/dot_general | solution.py:78
  155.6 17.2 %fusion.1 = f32[384,6144]{1,0:T(8,128)} fusion(bf16[2048,6144]{1,0:T(8,128)(2,1)} %param.20, bf16[384,2048]{1,0:T(8,128)(2,1)S(1)} %multiply_convert_fusion.clone.4), kind=kOutput, calls=%fused_computation.19 | convolution fusion | flops 9663676416 | bytes 36175872 | tf_op jit(solution)/shard_map/dot_general | solution.py:80
  172.8 16.3 %gather_fusion.2 = f32[512,6144]{1,0:T(8,128)} fusion(f32[384,6144]{1,0:T(8,128)} %fusion.1, s32[1024]{0:T(1024)S(1)} %get-tuple-element.213), kind=kCustom, calls=%fused_computation.2 | custom fusion | bytes 25167872 | tf_op jit(solution)/shard_map/gather | solution.py:83
  189.0 16.2 %gather_fusion.3 = f32[512,6144]{1,0:T(8,128)} fusion(f32[384,6144]{1,0:T(8,128)} %fusion.1, s32[1024]{0:T(1024)S(1)} %get-tuple-element.212), kind=kCustom, calls=%fused_computation.3 | custom fusion | bytes 25167872 | tf_op jit(solution)/shard_map/gather | solution.py:84
  205.2 14.0 %multiply_add_fusion.1 = f32[512,6144]{1,0:T(8,128)} fusion(f32[512,6144]{1,0:T(8,128)} %gather_fusion.3, f32[512,6144]{1,0:T(8,128)} %gather_fusion.2, f32[512]{0:T(512)S(1)} %bitcast.51, f32[512]{0:T(512)S(1)} %bitcast.50), kind=kLoop, calls=%fused_computation.8 | loop fusion | flops 9437184 | bytes 37752832 | tf_op jit(solution)/shard_map/add | solution.py:83
  219.3 0.6 copy-done.4
  219.9 132.4 %reduce-scatter.2.cloned.1.call-done = f32[512,384]{1,0:T(8,128)} async-done(((f32[512,6144]{1,0:T(8,128)}), f32[512,384]{1,0:T(8,128)}) %reduce-scatter.2.cloned.1.call-update) | async-done | bytes 786448 | tf_op jit(solution)/shard_map/reduce_scatter | solution.py:86
  352.3 1.3 multiply_reduce_fusion
  353.6 31.6 %psum.15 = f32[512]{0:T(512)S(1)} all-reduce(f32[512]{0:T(512)S(1)} %multiply_reduce_fusion), channel_id=1, replica_groups=mesh['groups'=2,'tensor'=16] {'tensor'}, use_global_device_ids=true, to_apply=%region_6.7 | all-reduce | flops 512 | bytes 4096 | tf_op jit(solution)/shard_map/psum | solution.py:88
  385.2 2.1 multiply_convert_fusion.1
  387.4 0.7 gather_fusion
  388.1 62.3 %all-gather.11.cloned.1.call-done = bf16[512,6144]{1,0:T(8,128)(2,1)} async-done(((bf16[512,384]{1,0:T(8,128)(2,1)}), bf16[512,6144]{1,0:T(8,128)(2,1)}) %all-gather.11.cloned.1.call-update) | async-done | bytes 6291472 | tf_op jit(solution)/shard_map/all_gather | solution.py:92
  450.4 18.6 %fusion.22 = (f32[512]{0:T(512)S(1)}, f32[512,2048]{1,0:T(8,128)S(1)}) fusion(bf16[512,6144]{1,0:T(8,128)(2,1)} %all-gather.11.cloned.1.call-done, bf16[6144,2048]{1,0:T(8,128)(2,1)} %param.21), kind=kOutput, calls=%fused_computation.73 | convolution fusion | flops 12885950464 | bytes 35653632 | tf_op jit(solution)/shard_map/dot_general | solution.py:91
  469.0 1.4 select_reduce_fusion.1
  470.4 18.8 %all-gather.5 = f32[16,1,512]{2,1,0:T(1,128)S(1)} all-gather(f32[1,1,512]{2,1,0:T(1,128)S(1)} %bitcast.49), channel_id=4, replica_groups=mesh['groups'=2,'tensor'=16] {'tensor'}, dimensions={0}, use_global_device_ids=true | all-gather | bytes 34816 | tf_op jit(solution)/shard_map/all_gather | solution.py:18
  489.3 17.5 %all-gather.4 = f32[16,1,512]{2,1,0:T(1,128)S(1)} all-gather(f32[1,1,512]{2,1,0:T(1,128)S(1)} %bitcast.48), channel_id=3, replica_groups=mesh['groups'=2,'tensor'=16] {'tensor'}, dimensions={0}, use_global_device_ids=true | all-gather | bytes 34816 | tf_op jit(solution)/shard_map/all_gather | solution.py:18
  506.8 18.8 %all-gather.3 = f32[16,1,512]{2,1,0:T(1,128)S(1)} all-gather(f32[1,1,512]{2,1,0:T(1,128)S(1)} %bitcast.47), channel_id=2, replica_groups=mesh['groups'=2,'tensor'=16] {'tensor'}, dimensions={0}, use_global_device_ids=true | all-gather | bytes 34816 | tf_op jit(solution)/shard_map/all_gather | solution.py:18
  525.6 1.4 while.19
  527.0 0.6 compare_select_fusion.6
  (99 shorter events, 2.0 us)
Async XLA Ops:
  6.5 380.9 %copy-start = (s32[8]{0:T(128)S(1)}, s32[8]{0:T(128)}, u32[]{:S(2)}) copy-start(s32[8]{0:T(128)} %param.23) | copy-start | bytes 100
  6.5 101.9 %all-gather.9.cloned.1.call-start = ((), (), s32[]{:S(2)}) async-start(), calls=%async_computation.1 | async-start | bytes 6684672 | tf_op jit(solution)/shard_map/all_gather | solution.py:75
  45.3 307.0 %reduce-scatter.2.cloned.1.call-start = ((), (), s32[]{:S(2)}) async-start(), calls=%async_computation.2 | async-start | bytes 13369344 | tf_op jit(solution)/shard_map/reduce_scatter | solution.py:86
  123.9 16.5 %copy-start.2 = (bf16[384,6144]{1,0:T(8,128)(2,1)S(1)}, bf16[384,6144]{1,0:T(8,128)(2,1)}, u32[]{:S(2)}) copy-start(bf16[384,6144]{1,0:T(8,128)(2,1)} %gather_fusion.1) | copy-start | bytes 14155780
  219.2 0.7 copy-start.4
  219.2 133.1 %copy-start.1 = (bf16[512,384]{1,0:T(8,128)(2,1)S(1)}, bf16[512,384]{1,0:T(8,128)(2,1)}, u32[]{:S(2)}) copy-start(bf16[512,384]{1,0:T(8,128)(2,1)} %param.13) | copy-start | bytes 1179652
  219.2 168.9 %copy-start.3 = (s32[512]{0:T(512)S(1)}, s32[512]{0:T(512)}, u32[]{:S(2)}) copy-start(s32[512]{0:T(512)} %param.22) | copy-start | bytes 6148
  219.2 231.2 %all-gather.11.cloned.1.call-start = ((), (), s32[]{:S(2)}) async-start(), calls=%async_computation.3 | async-start | bytes 6684672 | tf_op jit(solution)/shard_map/all_gather | solution.py:92
Sparse Core Ops, SparseCore 0:
  45.4 62.9 all-gather.8
  219.4 132.9 reduce-scatter.1
  387.5 62.9 all-gather.10

commit v2 on v1

--- a/solution.py
+++ b/solution.py
@@ -1,6 +1,9 @@
+import functools
 import jax
 import jax.numpy as jnp
 from jax import lax
+from jax.experimental import pallas as pl
+from jax.experimental.pallas import tpu as pltpu
 from jax.sharding import PartitionSpec as P
 
 D = 6144
@@ -45,7 +48,7 @@
     ).astype(jnp.bfloat16)
 
 
-def body(
+def plain_body(
     residual_in,
     norm_gain,
     final_gain,
@@ -117,6 +120,424 @@
     in_length = position % SEQ < lengths[position // SEQ]
     return jnp.where(in_length, own_rows, jnp.zeros_like(own_rows)).astype(jnp.float32)
 
+VMEM_BYTES = 56 * 1024 * 1024
+ORDER = (0, 1, 3, 2)
+
+
+def send(array, pairs):
+    return lax.ppermute(array, "tensor", pairs)
+
+
+def core_pairs():
+    return [(i, i ^ 1) for i in range(16)]
+
+
+def row_pairs():
+    return [(i, i ^ 2) for i in range(16)]
+
+
+def plane_pairs(k):
+    return [(i, ((i >> 2) + k) % 4 * 4 + (i & 3)) for i in range(16)]
+
+
+def summed_all(array):
+    array = array + send(array, core_pairs())
+    array = array + send(array, row_pairs())
+    others = [send(array, plane_pairs(k)) for k in (1, 2, 3)]
+    return array + others[0] + (others[1] + others[2])
+
+
+def one_hot(column, count):
+    return column[None, :] == jnp.arange(count, dtype=jnp.int32)[:, None]
+
+
+def params(steps):
+    return pltpu.CompilerParams(
+        dimension_semantics=("arbitrary",) * steps, vmem_limit_bytes=VMEM_BYTES
+    )
+
+
+def cost(rows, inner, cols, other_bytes):
+    return pl.CostEstimate(
+        flops=2 * rows * inner * cols,
+        transcendentals=0,
+        bytes_accessed=2 * inner * cols + other_bytes,
+    )
+
+
+def dispatch_kernel(slot_ref, x_ref, gain_ref, s0, s1, s2, s3, xc_ref):
+    x = x_ref[...]
+    scaled = (x.astype(jnp.float32) * gain_ref[...].astype(jnp.float32)).astype(jnp.bfloat16)
+    tokens = x.shape[0]
+    for k, out in enumerate((s0, s1, s2, s3)):
+        rows = out.shape[0]
+        spots = lax.broadcasted_iota(jnp.int32, (rows, tokens), 0)
+        chosen = jnp.where(slot_ref[k : k + 1, :] == spots, 1.0, 0.0).astype(jnp.bfloat16)
+        out[...] = jnp.dot(chosen, scaled, preferred_element_type=jnp.float32).astype(jnp.bfloat16)
+    rows = xc_ref.shape[0]
+    spots = lax.broadcasted_iota(jnp.int32, (rows, tokens), 0)
+    chosen = jnp.where(slot_ref[4:5, :] == spots, 1.0, 0.0).astype(jnp.bfloat16)
+    xc_ref[...] = jnp.dot(chosen, x, preferred_element_type=jnp.float32).astype(jnp.bfloat16)
+
+
+def dispatch(slot_rows, x, gain, slots, live_rows):
+    cols = x.shape[1]
+    block = jax.ShapeDtypeStruct((slots, cols), jnp.bfloat16)
+    return pl.pallas_call(
+        dispatch_kernel,
+        out_shape=[block] * 4 + [jax.ShapeDtypeStruct((live_rows, cols), jnp.bfloat16)],
+        compiler_params=pltpu.CompilerParams(vmem_limit_bytes=VMEM_BYTES),
+    )(slot_rows, x, gain)
+
+
+def place(where_ref, blocks, wide_ref):
+    cols = blocks[0].shape[1]
+    for b, block in enumerate(blocks):
+        at = pl.multiple_of(where_ref[1 + b] * cols, 128)
+        wide_ref[:, pl.ds(at, cols)] = block[...]
+
+
+def hidden_kernel(first, last, where_ref, *refs):
+    blocks, (wg, wu), refs = refs[:4], refs[4:6], refs[6:]
+    if not first:
+        g_in, u_in, refs = refs[0], refs[1], refs[2:]
+    if last:
+        inv, h_out, wide = refs
+    else:
+        g_out, u_out, wide = refs
+
+    @pl.when(pl.program_id(0) == 0)
+    def _():
+        place(where_ref, blocks, wide)
+
+    g = jnp.dot(wide[...], wg[...], preferred_element_type=jnp.float32)
+    u = jnp.dot(wide[...], wu[...], preferred_element_type=jnp.float32)
+    if not first:
+        g = g + g_in[...]
+        u = u + u_in[...]
+    if last:
+        g = g * inv[...]
+        u = u * inv[...]
+        h_out[...] = (g / (1.0 + jnp.exp(-g)) * u).astype(jnp.bfloat16)
+    else:
+        g_out[...] = g
+        u_out[...] = u
+
+
+def hidden_part(where, blocks, w_gate, w_up, sums, inv):
+    rows, cols = blocks[0].shape
+    width = w_gate.shape[1]
+    tile = 512
+    first, last = sums is None, inv is not None
+    whole = pl.BlockSpec((rows, cols), lambda n, w: (0, 0))
+    weight = pl.BlockSpec((4 * cols, tile), lambda n, w: (w[0], n))
+    out_tile = pl.BlockSpec((rows, tile), lambda n, w: (0, n))
+    ins, specs = [where, *blocks, w_gate, w_up], [whole] * 4 + [weight] * 2
+    aliases = {}
+    if not first:
+        ins += list(sums)
+        specs += [out_tile] * 2
+        if not last:
+            aliases = {7: 0, 8: 1}
+    if last:
+        ins.append(inv)
+        specs.append(pl.BlockSpec((rows, 1), lambda n, w: (0, 0)))
+        outs, out_specs = jax.ShapeDtypeStruct((rows, width), jnp.bfloat16), out_tile
+    else:
+        outs = [jax.ShapeDtypeStruct((rows, width), jnp.float32)] * 2
+        out_specs = [out_tile] * 2
+    return pl.pallas_call(
+        functools.partial(hidden_kernel, first, last),
+        out_shape=outs,
+        grid_spec=pltpu.PrefetchScalarGridSpec(
+            num_scalar_prefetch=1,
+            grid=(width // tile,),
+            in_specs=specs,
+            out_specs=out_specs,
+            scratch_shapes=[pltpu.VMEM((rows, 4 * cols), jnp.bfloat16)],
+        ),
+        input_output_aliases=aliases,
+        compiler_params=params(1),
+        cost_estimate=cost(rows, 4 * cols, 2 * width, 16 * rows * width),
+    )(*ins)
+
+
+def down_kernel(where_ref, h_ref, w_ref, gate_ref, o_own, o_row, o_core, o_far, total):
+    @pl.when(pl.program_id(0) == 0)
+    def _():
+        total[...] = jnp.zeros_like(total)
+
+    total[...] += jnp.dot(h_ref[...], w_ref[...], preferred_element_type=jnp.float32)
+
+    @pl.when(pl.program_id(0) == pl.num_programs(0) - 1)
+    def _():
+        cols = o_own.shape[1]
+        for b, out in enumerate((o_own, o_row, o_core, o_far)):
+            at = pl.multiple_of(where_ref[1 + b] * cols, 128)
+            out[...] = (total[:, pl.ds(at, cols)] * gate_ref[...]).astype(out.dtype)
+
+
+def down_part(where, hidden, w_down, gate_slot, cols):
+    rows, inner = hidden.shape
+    depth = 512
+    block = pl.BlockSpec((rows, cols), lambda j, w: (0, 0))
+    kinds = (jnp.float32, jnp.float32, jnp.bfloat16, jnp.bfloat16)
+    return pl.pallas_call(
+        down_kernel,
+        out_shape=[jax.ShapeDtypeStruct((rows, cols), kind) for kind in kinds],
+        grid_spec=pltpu.PrefetchScalarGridSpec(
+            num_scalar_prefetch=1,
+            grid=(inner // depth,),
+            in_specs=[
+                pl.BlockSpec((rows, depth), lambda j, w: (0, j)),
+                pl.BlockSpec((depth, 4 * cols), lambda j, w: (j, w[0])),
+                pl.BlockSpec((rows, 1), lambda j, w: (0, 0)),
+            ],
+            out_specs=[block] * 4,
+            scratch_shapes=[pltpu.VMEM((rows, 4 * cols), jnp.float32)],
+        ),
+        compiler_params=params(1),
+        cost_estimate=cost(rows, inner, 4 * cols, 24 * rows * cols),
+    )(where, hidden, w_down, gate_slot)
+
+
+def mix_kernel(slot_ref, x_ref, gain_ref, e0, e1, e2, e3, out_ref, squares_ref):
+    rows = x_ref.shape[0]
+    mixture = x_ref[...].astype(jnp.float32)
+    moe = jnp.zeros_like(mixture)
+    for j, part in enumerate((e0, e1, e2, e3)):
+        slots = part.shape[0]
+        spots = lax.broadcasted_iota(jnp.int32, (rows, slots), 1)
+        chosen = jnp.where(slot_ref[:, j : j + 1] == spots, 1.0, 0.0).astype(jnp.bfloat16)
+        moe = moe + jnp.dot(chosen, part[...], preferred_element_type=jnp.float32)
+    mixture = mixture + moe
+    out_ref[...] = (mixture * gain_ref[...].astype(jnp.float32)).astype(jnp.bfloat16)
+    squares_ref[...] = jnp.sum(mixture * mixture, axis=1, keepdims=True)
+
+
+def mix(slot_cols, x, gain, parts):
+    rows, cols = x.shape
+    return pl.pallas_call(
+        mix_kernel,
+        out_shape=[
+            jax.ShapeDtypeStruct((rows, cols), jnp.bfloat16),
+            jax.ShapeDtypeStruct((rows, 1), jnp.float32),
+        ],
+        compiler_params=pltpu.CompilerParams(vmem_limit_bytes=VMEM_BYTES),
+    )(slot_cols, x, gain, *parts)
+
+
+def vocab_kernel(first, last, where_ref, *refs):
+    blocks, w_ref, refs = refs[:4], refs[4], refs[5:]
+    if not first:
+        sum_in, refs = refs[0], refs[1:]
+    if last:
+        inv, local_ids, out, wide, top, total, picked = refs
+    else:
+        out, wide = refs
+    n = pl.program_id(0)
+
+    @pl.when(n == 0)
+    def _():
+        place(where_ref, blocks, wide)
+
+    value = jnp.dot(wide[...], w_ref[...], preferred_element_type=jnp.float32)
+    if not first:
+        value = value + sum_in[...]
+    if not last:
+        out[...] = value
+        return
+    logits = value * inv[...]
+    rows, tile = logits.shape
+    column = n * tile + lax.broadcasted_iota(jnp.int32, (rows, tile), 1)
+    tile_pick = jnp.sum(jnp.where(column == local_ids[...], logits, 0.0), axis=1, keepdims=True)
+    tile_top = jnp.max(logits, axis=1, keepdims=True)
+
+    @pl.when(n == 0)
+    def _():
+        top[...] = tile_top
+        total[...] = jnp.sum(jnp.exp(logits - tile_top), axis=1, keepdims=True)
+        picked[...] = tile_pick
+
+    @pl.when(n > 0)
+    def _():
+        new_top = jnp.maximum(top[...], tile_top)
+        total[...] = total[...] * jnp.exp(top[...] - new_top) + jnp.sum(
+            jnp.exp(logits - new_top), axis=1, keepdims=True
+        )
+        top[...] = new_top
+        picked[...] = picked[...] + tile_pick
+
+    @pl.when(n == pl.num_programs(0) - 1)
+    def _():
+        lane = lax.broadcasted_iota(jnp.int32, out.shape, 1)
+        out[...] = jnp.where(lane == 0, top[...], jnp.where(lane == 1, total[...], picked[...]))
+
+
+def vocab_part(where, blocks, lm_head, sums, inv, local_ids):
+    rows, cols = blocks[0].shape
+    width = lm_head.shape[1]
+    tile = 512
+    first, last = sums is None, inv is not None
+    whole = pl.BlockSpec((rows, cols), lambda n, w: (0, 0))
+    out_tile = pl.BlockSpec((rows, tile), lambda n, w: (0, n))
+    ins = [where, *blocks, lm_head]
+    specs = [whole] * 4 + [pl.BlockSpec((4 * cols, tile), lambda n, w: (w[0], n))]
+    aliases = {}
+    if not first:
+        ins.append(sums)
+        specs.append(out_tile)
+        if not last:
+            aliases = {6: 0}
+    scratch = [pltpu.VMEM((rows, 4 * cols), jnp.bfloat16)]
+    if last:
+        ins += [inv, local_ids]
+        specs += [pl.BlockSpec((rows, 1), lambda n, w: (0, 0))] * 2
+        outs = jax.ShapeDtypeStruct((rows, 128), jnp.float32)
+        out_specs = pl.BlockSpec((rows, 128), lambda n, w: (0, 0))
+        scratch += [pltpu.VMEM((rows, 1), jnp.float32)] * 3
+    else:
+        outs, out_specs = jax.ShapeDtypeStruct((rows, width), jnp.float32), out_tile
+    return pl.pallas_call(
+        functools.partial(vocab_kernel, first, last),
+        out_shape=outs,
+        grid_spec=pltpu.PrefetchScalarGridSpec(
+            num_scalar_prefetch=1,
+            grid=(width // tile,),
+            in_specs=specs,
+            out_specs=out_specs,
+            scratch_shapes=scratch,
+        ),
+        input_output_aliases=aliases,
+        compiler_params=params(1),
+        cost_estimate=cost(rows, 4 * cols, width, 8 * rows * width),
+    )(*ins)
+
+
+def spread(by_offset):
+    arrived = {0: by_offset[0]}
+    arrived[1] = send(by_offset[1], plane_pairs(1))
+    arrived[3] = send(by_offset[3], plane_pairs(3))
+    later, _, _ = lax.optimization_barrier((by_offset[2], arrived[1], arrived[3]))
+    arrived[2] = send(later, plane_pairs(2))
+    chunks = {}
+    for k in ORDER:
+        own = arrived[k]
+        row = send(own, row_pairs())
+        chunks[k] = (own, row, send(own, core_pairs()), send(row, core_pairs()))
+    return chunks
+
+
+def fast_body(
+    residual_in,
+    norm_gain,
+    final_gain,
+    expert_ids,
+    gate_values,
+    w_gate,
+    w_up,
+    w_down,
+    lm_head,
+    target_ids,
+    lengths,
+    live_rows,
+    slots,
+):
+    tokens, cols = residual_in.shape
+    me = lax.axis_index("tensor")
+    plane, row, core = me // 4, me // 2 % 2, me % 2
+    offsets = [row * 2 + core, (1 - row) * 2 + core, row * 2 + 1 - core, (1 - row) * 2 + 1 - core]
+    where = {k: jnp.stack([(plane + k) % 4, *offsets]).astype(jnp.int32) for k in range(4)}
+
+    place_in = jnp.arange(tokens, dtype=jnp.int32)
+    cands = lengths.shape[0]
+    cand = jnp.arange(cands, dtype=jnp.int32)
+    starts = jnp.sum(jnp.where(cand[None, :] < cand[:, None], lengths[None, :], 0), axis=1)
+    step = jnp.arange(SEQ, dtype=jnp.int32)
+    live = (step[None, :] < lengths[:, None]).reshape(-1)
+    packed = jnp.where(live, (starts[:, None] + step[None, :]).reshape(-1), -1)
+
+    expert_at = (plane + jnp.arange(EXPERTS, dtype=jnp.int32)) % EXPERTS
+    hit = (expert_ids[:, :, None] == expert_at[None, None, :]) & live[:, None, None]
+    used = jnp.any(hit, axis=1)
+    gate = jnp.sum(jnp.where(hit, gate_values[:, :, None], 0.0), axis=1)
+    earlier = (place_in[None, :] < place_in[:, None]).astype(jnp.bfloat16)
+    rank = jnp.dot(earlier, used.astype(jnp.bfloat16), preferred_element_type=jnp.float32)
+    slot = jnp.where(used, rank.astype(jnp.int32), -1)
+
+    slot_rows = jnp.concatenate(
+        [slot.T, packed[None, :], jnp.zeros((3, tokens), jnp.int32)], axis=0
+    )
+    *picked_rows, x_live = dispatch(slot_rows, residual_in, norm_gain[None, :], slots, live_rows)
+    chunks = spread(picked_rows)
+
+    stream = residual_in.astype(jnp.float32)
+    in_total = summed_all(jnp.sum(stream * stream, axis=1))
+    in_scale = 1.0 / jnp.sqrt(in_total / D + epsilon)
+    own_slot = one_hot(slot[:, 0], slots)
+    inv_slot = jnp.sum(jnp.where(own_slot, in_scale[None, :], 0.0), axis=1, keepdims=True)
+    gate_slot = jnp.sum(jnp.where(own_slot, gate[:, 0][None, :], 0.0), axis=1, keepdims=True)
+    live_at = one_hot(packed, live_rows)
+    slot_live = (
+        jnp.sum(jnp.where(live_at[:, :, None], slot[None, :, :] + 1, 0), axis=1) - 1
+    )
+    slot_live = jnp.stack([slot_live[:, (4 - k) % 4] for k in range(4)], axis=1)
+    target_live = jnp.sum(jnp.where(live_at, target_ids[None, :], 0), axis=1, keepdims=True)
+
+    sums = None
+    for k in ORDER:
+        last = k == ORDER[-1]
+        sums = hidden_part(
+            where[(4 - k) % 4], chunks[k], w_gate, w_up, sums, inv_slot if last else None
+        )
+    hidden = sums
+
+    parts = {}
+    for k in (2, 1, 3, 0):
+        own, across, near, far = down_part(where[k], hidden, w_down, gate_slot, cols)
+        near = send(near, core_pairs())
+        far = send(far, core_pairs())
+        across = send((across + far.astype(jnp.float32)).astype(jnp.bfloat16), row_pairs())
+        own = own + near.astype(jnp.float32) + across.astype(jnp.float32)
+        own = own.astype(jnp.bfloat16)
+        parts[k] = send(own, plane_pairs(k)) if k else own
+
+    scaled, squares = mix(slot_live, x_live, final_gain[None, :], [parts[k] for k in range(4)])
+    chunks = spread([scaled] * 4)
+    out_total = summed_all(squares.reshape(-1))
+    out_scale = (1.0 / jnp.sqrt(out_total / D + epsilon))[:, None]
+    local_ids = target_live - me * lm_head.shape[1]
+    sums = None
+    for k in ORDER:
+        last = k == ORDER[-1]
+        sums = vocab_part(
+            where[(4 - k) % 4], chunks[k], lm_head, sums, out_scale if last else None, local_ids
+        )
+    stats = sums[:, :3].T
+
+    def joined(a, b):
+        top = jnp.maximum(a[0], b[0])
+        return jnp.stack(
+            [top, a[1] * jnp.exp(a[0] - top) + b[1] * jnp.exp(b[0] - top), a[2] + b[2]]
+        )
+
+    stats = joined(stats, send(stats, core_pairs()))
+    stats = joined(stats, send(stats, row_pairs()))
+    others = [send(stats, plane_pairs(k)) for k in (1, 2, 3)]
+    stats = joined(joined(stats, others[0]), joined(others[1], others[2]))
+    logprob = stats[2] - stats[0] - jnp.log(stats[1])
+    rows_dev = tokens // lax.axis_size("tensor")
+    own_packed = lax.dynamic_slice_in_dim(packed, me * rows_dev, rows_dev)
+    mine = own_packed[:, None] == jnp.arange(live_rows, dtype=jnp.int32)[None, :]
+    return jnp.sum(jnp.where(mine, logprob[None, :], 0.0), axis=1)
+
+
+def body(*args):
+    if lax.axis_size("tensor") != 16:
+        return plain_body(*args)
+    tokens = args[0].shape[0]
+    return fast_body(*args, live_rows=tokens, slots=CAP)
+
 
 def solution(mesh):
     return jax.shard_map(

time: 535 us -> 319 us (0.60)
  waiting for transfers between devices: 253 us -> 105 us
  Pallas kernels: 0 us -> 124 us
  blocking collectives: 122 us -> 0 us
  matrix products: 67.5 us -> 0.23 us
  starting transfers between devices: 0.09 us -> 55.1 us
  local copies, waits for them, and re-layouts: 51.2 us -> 16.3 us
  other arithmetic: 26.8 us -> 13.4 us
  between operations: 13.3 us -> 0.66 us
    reduce_scatter x1 -> x0, waiting for transfers between devices: 132 us -> none  [body(): lax.psum_scatter(weighted, 'tensor', scatter_dimension=1, tiled=True)]
    pallas_call x0 -> x14, Pallas kernels: none -> 124 us  [the longest x4 47.4 us: hidden_part(): pl.pallas_call(functools.partial(hidden_kernel, first, last), out_shape=o...]
    all_gather x2 -> x0, waiting for transfers between devices: 121 us -> none  [the longest x1 62.3 us: body(): lax.all_gather(normed_out, 'tensor', axis=1, tiled=True)]
    ppermute x0 -> x60, waiting for transfers between devices: none -> 105 us  [send(): return lax.ppermute(array, 'tensor', pairs)]
    dot_general x4 -> x1, matrix products: 67.5 us -> 0.23 us  [fast_body(): jnp.dot(earlier, used.astype(jnp.bfloat16), preferred_element_type=jnp.fl...]
    psum x2 -> x0, blocking collectives: 66.5 us -> none  [the longest x1 34.9 us: body(): in_total = lax.psum(jnp.sum(stream * stream, axis=1), 'tensor')]
    all_gather x3 -> x0, blocking collectives: 55.2 us -> none  [combined_all(): everything = jax.tree.map(lambda part: lax.all_gather(part, axis), array)]
    ppermute x0 -> x60, starting transfers between devices: none -> 55.1 us  [send(): return lax.ppermute(array, 'tensor', pairs)]
  transfers between devices with their start and end apart: 3 -> 60, of which waited for: 3 -> 21; matrix products, arithmetic and copies ran while one was open for 1% -> 5% of each run, Pallas kernels for 0% -> 25%
where the time goes in v2:
time: 319 us; the launch traced here: 315 us
  Pallas kernels  124 us (39%)
  waiting for transfers between devices  105 us (33%)
  starting transfers between devices  55.1 us (17%)
  local copies, waits for them, and re-layouts  16.3 us (5%)
  other arithmetic  13.4 us (4%)
    ppermute x60, waiting for transfers between devices, send(): return lax.ppermute(array, 'tensor', pairs)  105 us
    ppermute x60, starting transfers between devices, send(): return lax.ppermute(array, 'tensor', pairs)  55.1 us
    pallas_call x4, Pallas kernels, hidden_part(): pl.pallas_call(functools.partial(hidden_kernel, first, last), out_shape=o...  47.4 us
    pallas_call x4, Pallas kernels, vocab_part(): pl.pallas_call(functools.partial(vocab_kernel, first, last), out_shape=ou...  37.7 us
    pallas_call x4, Pallas kernels, down_part(): pl.pallas_call(down_kernel, out_shape=[jax.ShapeDtypeStruct((rows, cols),...  32 us
    unnamed x92, local copies, waits for them, and re-layouts  6.42 us
  transfers between devices with their start and end apart: 60, of which 21 were waited for; matrix products, arithmetic and copies ran while one was open for 5% of the time, Pallas kernels for 25%

profile of v2, /device:TPU:0, one launch (start us, length us, event | category | flops | bytes accessed | tf_op | source)
XLA Modules:
  0.0 314.6 jit_solution(3927692923576939987)
XLA Ops:
  5.4 3.0 shard_map.109
  18.6 3.3 %collective-permute-done.16 = f32[512]{0:T(512)S(1)} collective-permute-done((f32[512]{0:T(512)S(1)}, f32[512]{0:T(512)S(1)}, u32[]{:S(2)}, u32[]{:S(2)}) %collective-permute-start.16) | collective-permute-done | bytes 2080 | tf_op jit(solution)/shard_map/ppermute | solution.py:128
  24.2 5.8 %collective-permute-start.19 = (f32[512]{0:T(512)S(1)}, f32[512]{0:T(512)S(1)}, u32[]{:S(2)}, u32[]{:S(2)}) collective-permute-start(f32[512]{0:T(512)S(1)} %add.238), channel_id=1, source_target_pairs={{0,12},{1,13},{2,14},{3,15},{4,0},{5,1},{6,2},{7,3},{8,4},{9,5},{1... | collective-permute-start | bytes 6152 | tf_op jit(solution)/shard_map/ppermute | solution.py:128
  37.2 5.3 %collective-permute-done.9.refs_1_ = bf16[384,384]{1,0:T(8,128)(2,1)S(1)} collective-permute-done((bf16[384,384]{1,0:T(8,128)(2,1)S(1)}, bf16[384,384]{1,0:T(8,128)(2,1)S(1)}, u32[]{:S(2)}, u32[]{:S(2)}) %collective-permute-start.9) | collective-permute-done | bytes 294944 | tf_op jit(solution)/shard_map/ppermute | solution.py:128
  42.6 4.3 %collective-permute-done.2.refs_0_ = bf16[384,384]{1,0:T(8,128)(2,1)S(1)} collective-permute-done((bf16[384,384]{1,0:T(8,128)(2,1)}, bf16[384,384]{1,0:T(8,128)(2,1)S(1)}, u32[]{:S(2)}, u32[]{:S(2)}) %collective-permute-start.2) | collective-permute-done | bytes 294944 | tf_op jit(solution)/shard_map/ppermute | solution.py:128
  47.4 10.7 %shard_map.110 = (f32[384,2048]{1,0:T(8,128)}, f32[384,2048]{1,0:T(8,128)}) custom-call(s32[5]{0:T(128)} %stack.71.where_ref, bf16[384,384]{1,0:T(8,128)(2,1)} %get-tuple-element.41.refs_0_, bf16[384,384]{1,0:T(8,128)(2,1)} %copy-done.35, bf16[384,384]{1,0:T(8,128)(2,1)} %copy-done.36, bf16[384,384]{1,0:T(8,128)(2,1)} %copy-done.37, ...), custom_call_target="tpu_custom_call" | custom-call | flops 4831838208 | bytes 25165824 | tf_op jit(solution)/shard_map/pallas_call | solution.py:249
  59.5 12.4 %shard_map.111 = (f32[384,2048]{1,0:T(8,128)}, f32[384,2048]{1,0:T(8,128)}) custom-call(s32[5]{0:T(128)} %stack.75.where_ref, bf16[384,384]{1,0:T(8,128)(2,1)} %copy-done.21, bf16[384,384]{1,0:T(8,128)(2,1)} %copy-done.23, bf16[384,384]{1,0:T(8,128)(2,1)} %copy-done.27, bf16[384,384]{1,0:T(8,128)(2,1)} %copy-done.29, ...), custom_call_target="tpu_custom_call", output_to_operand_aliasing={{0}: (7, {}), {1}: (8, {})} | custom-call | flops 4831838208 | bytes 25165824 | tf_op jit(solution)/shard_map/pallas_call | solution.py:249
  72.8 12.4 %shard_map.112 = (f32[384,2048]{1,0:T(8,128)}, f32[384,2048]{1,0:T(8,128)}) custom-call(s32[5]{0:T(128)} %stack.73.where_ref, bf16[384,384]{1,0:T(8,128)(2,1)} %copy-done.20, bf16[384,384]{1,0:T(8,128)(2,1)} %copy-done.24, bf16[384,384]{1,0:T(8,128)(2,1)} %copy-done.25, bf16[384,384]{1,0:T(8,128)(2,1)} %copy-done.31, ...), custom_call_target="tpu_custom_call", output_to_operand_aliasing={{0}: (7, {}), {1}: (8, {})} | custom-call | flops 4831838208 | bytes 25165824 | tf_op jit(solution)/shard_map/pallas_call | solution.py:249
  86.0 11.9 %shard_map.113.h_ref = bf16[384,2048]{1,0:T(8,128)(2,1)} custom-call(s32[5]{0:T(128)} %stack.68.where_ref, bf16[384,384]{1,0:T(8,128)(2,1)} %copy-done.22, bf16[384,384]{1,0:T(8,128)(2,1)} %copy-done.26, bf16[384,384]{1,0:T(8,128)(2,1)} %copy-done.28, bf16[384,384]{1,0:T(8,128)(2,1)} %copy-done.30, bf16[6144,2048]{1,0:T(8,128)(2,1)} %refs_4_.11, ...), custom_call_target="tpu_custom_call" | custom-call | flops 4831838208 | bytes 25165824 | tf_op jit(solution)/shard_map/pallas_call | solution.py:249
  97.9 7.9 %shard_map.117 = (f32[384,384]{1,0:T(8,128)}, f32[384,384]{1,0:T(8,128)}, bf16[384,384]{1,0:T(8,128)(2,1)}, bf16[384,384]{1,0:T(8,128)(2,1)}) custom-call(s32[5]{0:T(128)} %stack.75.where_ref, bf16[384,2048]{1,0:T(8,128)(2,1)} %shard_map.113.h_ref, bf16[2048,6144]{1,0:T(8,128)(2,1)} %w_ref.7, f32[384,1]{1,0:T(8,128)} %broadcast_in_dim.168.gate_ref), custom_call_target="tpu_custom_call" | custom-call | flops 2415919104 | bytes 9830400 | tf_op jit(solution)/shard_map/pallas_call | solution.py:285
  105.8 8.0 %shard_map.116 = (f32[384,384]{1,0:T(8,128)}, f32[384,384]{1,0:T(8,128)}, bf16[384,384]{1,0:T(8,128)(2,1)}, bf16[384,384]{1,0:T(8,128)(2,1)}) custom-call(s32[5]{0:T(128)} %stack.68.where_ref, bf16[384,2048]{1,0:T(8,128)(2,1)} %shard_map.113.h_ref, bf16[2048,6144]{1,0:T(8,128)(2,1)} %w_ref.7, f32[384,1]{1,0:T(8,128)} %broadcast_in_dim.168.gate_ref), custom_call_target="tpu_custom_call" | custom-call | flops 2415919104 | bytes 9830400 | tf_op jit(solution)/shard_map/pallas_call | solution.py:285
  114.4 7.9 %shard_map.115 = (f32[384,384]{1,0:T(8,128)}, f32[384,384]{1,0:T(8,128)}, bf16[384,384]{1,0:T(8,128)(2,1)}, bf16[384,384]{1,0:T(8,128)(2,1)}) custom-call(s32[5]{0:T(128)} %stack.73.where_ref, bf16[384,2048]{1,0:T(8,128)(2,1)} %shard_map.113.h_ref, bf16[2048,6144]{1,0:T(8,128)(2,1)} %w_ref.7, f32[384,1]{1,0:T(8,128)} %broadcast_in_dim.168.gate_ref), custom_call_target="tpu_custom_call" | custom-call | flops 2415919104 | bytes 9830400 | tf_op jit(solution)/shard_map/pallas_call | solution.py:285
  122.5 8.1 %shard_map.114 = (f32[384,384]{1,0:T(8,128)}, f32[384,384]{1,0:T(8,128)}, bf16[384,384]{1,0:T(8,128)(2,1)}, bf16[384,384]{1,0:T(8,128)(2,1)}) custom-call(s32[5]{0:T(128)} %stack.71.where_ref, bf16[384,2048]{1,0:T(8,128)(2,1)} %shard_map.113.h_ref, bf16[2048,6144]{1,0:T(8,128)(2,1)} %w_ref.7, f32[384,1]{1,0:T(8,128)} %broadcast_in_dim.168.gate_ref), custom_call_target="tpu_custom_call" | custom-call | flops 2415919104 | bytes 9830400 | tf_op jit(solution)/shard_map/pallas_call | solution.py:285
  137.1 5.9 %collective-permute-done.33 = bf16[384,384]{1,0:T(8,128)(2,1)S(1)} collective-permute-done((bf16[384,384]{1,0:T(8,128)(2,1)S(1)}, bf16[384,384]{1,0:T(8,128)(2,1)S(1)}, u32[]{:S(2)}, u32[]{:S(2)}) %collective-permute-start.33) | collective-permute-done | bytes 294944 | tf_op jit(solution)/shard_map/ppermute | solution.py:128
  145.2 4.1 %collective-permute-done.29 = bf16[384,384]{1,0:T(8,128)(2,1)S(1)} collective-permute-done((bf16[384,384]{1,0:T(8,128)(2,1)S(1)}, bf16[384,384]{1,0:T(8,128)(2,1)S(1)}, u32[]{:S(2)}, u32[]{:S(2)}) %collective-permute-start.29) | collective-permute-done | bytes 294944 | tf_op jit(solution)/shard_map/ppermute | solution.py:128
  152.1 3.5 %collective-permute-done.25 = bf16[384,384]{1,0:T(8,128)(2,1)S(1)} collective-permute-done((bf16[384,384]{1,0:T(8,128)(2,1)S(1)}, bf16[384,384]{1,0:T(8,128)(2,1)S(1)}, u32[]{:S(2)}, u32[]{:S(2)}) %collective-permute-start.25) | collective-permute-done | bytes 294944 | tf_op jit(solution)/shard_map/ppermute | solution.py:128
  157.5 3.9 %collective-permute-done.22 = bf16[384,384]{1,0:T(8,128)(2,1)S(1)} collective-permute-done((bf16[384,384]{1,0:T(8,128)(2,1)S(1)}, bf16[384,384]{1,0:T(8,128)(2,1)S(1)}, u32[]{:S(2)}, u32[]{:S(2)}) %collective-permute-start.22) | collective-permute-done | bytes 294944 | tf_op jit(solution)/shard_map/ppermute | solution.py:128
  162.3 13.3 %collective-permute-done.30.e2 = bf16[384,384]{1,0:T(8,128)(2,1)S(1)} collective-permute-done((bf16[384,384]{1,0:T(8,128)(2,1)S(1)}, bf16[384,384]{1,0:T(8,128)(2,1)S(1)}, u32[]{:S(2)}, u32[]{:S(2)}) %collective-permute-start.30) | collective-permute-done | bytes 294944 | tf_op jit(solution)/shard_map/ppermute | solution.py:128
  176.5 3.6 %shard_map.118 = (bf16[512,384]{1,0:T(8,128)(2,1)}, f32[512,1]{1,0:T(8,128)}) custom-call(s32[512,4]{1,0:T(8,128)} %copy.68.slot_ref, bf16[512,384]{1,0:T(8,128)(2,1)} %get-tuple-element.36.x_ref, bf16[1,384]{1,0:T(2,128)(2,1)} %broadcast_in_dim.152.gain_ref, bf16[384,384]{1,0:T(8,128)(2,1)} %add_convert_fusion.6.e0, bf16[384,384]{1,0:T(8,128)(2,1)} %copy-done.34, ...), custom_call_target="tpu_custom_call" | custom-call | tf_op jit(solution)/shard_map/pallas_call | solution.py:320
  185.4 8.7 %collective-permute-done.35.refs_0_ = bf16[512,384]{1,0:T(8,128)(2,1)S(1)} collective-permute-done((bf16[512,384]{1,0:T(8,128)(2,1)}, bf16[512,384]{1,0:T(8,128)(2,1)S(1)}, u32[]{:S(2)}, u32[]{:S(2)}) %collective-permute-start.35) | collective-permute-done | bytes 393248 | tf_op jit(solution)/shard_map/ppermute | solution.py:128
  194.1 5.4 %collective-permute-done.36.refs_0_ = bf16[512,384]{1,0:T(8,128)(2,1)S(1)} collective-permute-done((bf16[512,384]{1,0:T(8,128)(2,1)}, bf16[512,384]{1,0:T(8,128)(2,1)S(1)}, u32[]{:S(2)}, u32[]{:S(2)}) %collective-permute-start.36) | collective-permute-done | bytes 393248 | tf_op jit(solution)/shard_map/ppermute | solution.py:128
  206.6 4.0 %collective-permute-done.51 = f32[512]{0:T(512)S(1)} collective-permute-done((f32[512]{0:T(512)S(1)}, f32[512]{0:T(512)S(1)}, u32[]{:S(2)}, u32[]{:S(2)}) %collective-permute-start.51) | collective-permute-done | bytes 2080 | tf_op jit(solution)/shard_map/ppermute | solution.py:128
  211.2 4.9 %collective-permute-done.52 = f32[512]{0:T(512)S(1)} collective-permute-done((f32[512]{0:T(512)S(1)}, f32[512]{0:T(512)S(1)}, u32[]{:S(2)}, u32[]{:S(2)}) %collective-permute-start.52) | collective-permute-done | bytes 2080 | tf_op jit(solution)/shard_map/ppermute | solution.py:128
  216.1 5.3 %collective-permute-start.53 = (f32[512]{0:T(512)S(1)}, f32[512]{0:T(512)}, u32[]{:S(2)}, u32[]{:S(2)}) collective-permute-start(f32[512]{0:T(512)S(1)} %add.256), channel_id=1, source_target_pairs={{0,8},{1,9},{2,10},{3,11},{4,12},{5,13},{6,14},{7,15},{8,0},{9,1},... | collective-permute-start | bytes 6152 | tf_op jit(solution)/shard_map/ppermute | solution.py:128
  232.0 6.4 %collective-permute-done.41.refs_1_ = bf16[512,384]{1,0:T(8,128)(2,1)S(1)} collective-permute-done((bf16[512,384]{1,0:T(8,128)(2,1)S(1)}, bf16[512,384]{1,0:T(8,128)(2,1)S(1)}, u32[]{:S(2)}, u32[]{:S(2)}) %collective-permute-start.41) | collective-permute-done | bytes 393248 | tf_op jit(solution)/shard_map/ppermute | solution.py:128
  238.4 8.6 %shard_map.119.refs_5_ = f32[512,2048]{1,0:T(8,128)} custom-call(s32[5]{0:T(128)} %stack.71.where_ref, bf16[512,384]{1,0:T(8,128)(2,1)} %get-tuple-element.65.refs_0_, bf16[512,384]{1,0:T(8,128)(2,1)} %copy-done.11, bf16[512,384]{1,0:T(8,128)(2,1)} %copy-done.12, bf16[512,384]{1,0:T(8,128)(2,1)} %collective-permute-done.49.refs_3_, bf16[6144,2048]{1,0:T(8,128)(2,1)} %refs_4_.15), custom_call_target="tpu_custom_call" | custom-call | flops 3221225472 | bytes 14680064 | tf_op jit(solution)/shard_map/pallas_call | solution.py:401
  247.8 9.5 %shard_map.120.refs_5_ = f32[512,2048]{1,0:T(8,128)} custom-call(s32[5]{0:T(128)} %stack.75.where_ref, bf16[512,384]{1,0:T(8,128)(2,1)} %copy-done.8, bf16[512,384]{1,0:T(8,128)(2,1)} %copy-done.10, bf16[512,384]{1,0:T(8,128)(2,1)} %copy-done.15, bf16[512,384]{1,0:T(8,128)(2,1)} %collective-permute-done.46.refs_3_, ...), custom_call_target="tpu_custom_call", output_to_operand_aliasing={{}: (6, {})} | custom-call | flops 3221225472 | bytes 14680064 | tf_op jit(solution)/shard_map/pallas_call | solution.py:401
  258.9 9.5 %shard_map.121.refs_5_ = f32[512,2048]{1,0:T(8,128)} custom-call(s32[5]{0:T(128)} %stack.73.where_ref, bf16[512,384]{1,0:T(8,128)(2,1)} %copy-done.7, bf16[512,384]{1,0:T(8,128)(2,1)} %copy-done.13, bf16[512,384]{1,0:T(8,128)(2,1)} %copy-done.16, bf16[512,384]{1,0:T(8,128)(2,1)} %copy-done.18, ...), custom_call_target="tpu_custom_call", output_to_operand_aliasing={{}: (6, {})} | custom-call | flops 3221225472 | bytes 14680064 | tf_op jit(solution)/shard_map/pallas_call | solution.py:401
  269.9 10.1 %shard_map.122 = f32[512,128]{1,0:T(8,128)} custom-call(s32[5]{0:T(128)} %stack.68.where_ref, bf16[512,384]{1,0:T(8,128)(2,1)} %copy-done.9, bf16[512,384]{1,0:T(8,128)(2,1)} %copy-done.14, bf16[512,384]{1,0:T(8,128)(2,1)} %copy-done.17, bf16[512,384]{1,0:T(8,128)(2,1)} %copy-done.19, bf16[6144,2048]{1,0:T(8,128)(2,1)} %refs_4_.15, ...), custom_call_target="tpu_custom_call" | custom-call | flops 3221225472 | bytes 14680064 | tf_op jit(solution)/shard_map/pallas_call | solution.py:401
  283.3 8.6 %collective-permute-done.56 = f32[3,512]{0,1:T(8,128)S(1)} collective-permute-done((f32[3,512]{0,1:T(8,128)S(1)}, f32[3,512]{0,1:T(8,128)S(1)}, u32[]{:S(2)}, u32[]{:S(2)}) %collective-permute-start.56) | collective-permute-done | bytes 6176 | tf_op jit(solution)/shard_map/ppermute | solution.py:128
  297.7 5.8 %collective-permute-done.57 = f32[3,512]{0,1:T(8,128)S(1)} collective-permute-done((f32[3,512]{0,1:T(8,128)S(1)}, f32[3,512]{0,1:T(8,128)S(1)}, u32[]{:S(2)}, u32[]{:S(2)}) %collective-permute-start.57) | collective-permute-done | bytes 6176 | tf_op jit(solution)/shard_map/ppermute | solution.py:128
  303.5 9.8 %collective-permute-done.58 = f32[3,512]{0,1:T(8,128)S(1)} collective-permute-done((f32[3,512]{0,1:T(8,128)S(1)}, f32[3,512]{0,1:T(8,128)S(1)}, u32[]{:S(2)}, u32[]{:S(2)}) %collective-permute-start.58) | collective-permute-done | bytes 6176 | tf_op jit(solution)/shard_map/ppermute | solution.py:128
  (253 shorter events, 81.8 us)
Async XLA Ops:
  8.4 24.9 %collective-permute-start.12 = (bf16[384,384]{1,0:T(8,128)(2,1)}, bf16[384,384]{1,0:T(8,128)(2,1)S(1)}, u32[]{:S(2)}, u32[]{:S(2)}) collective-permute-start(bf16[384,384]{1,0:T(8,128)(2,1)} %get-tuple-element.41.refs_0_), channel_id=1, source_target_pairs={{0,2},{1,3},{2,0},{3,1},{4,6},{5,7},{6,4},{7,5},{8,10},{9,11},{10,... | collective-permute-start | bytes 884744 | tf_op jit(solution)/shard_map/ppermute | solution.py:128
  13.0 19.6 %collective-permute-start.1 = (bf16[384,384]{1,0:T(8,128)(2,1)}, bf16[384,384]{1,0:T(8,128)(2,1)S(1)}, u32[]{:S(2)}, u32[]{:S(2)}) collective-permute-start(bf16[384,384]{1,0:T(8,128)(2,1)} %get-tuple-element.39), channel_id=1, source_target_pairs={{0,12},{1,13},{2,14},{3,15},{4,0},{5,1},{6,2},{7,3},{8,4},{9,5},{1... | collective-permute-start | bytes 884744 | tf_op jit(solution)/shard_map/ppermute | solution.py:128
  32.6 14.2 %collective-permute-start.2 = (bf16[384,384]{1,0:T(8,128)(2,1)}, bf16[384,384]{1,0:T(8,128)(2,1)S(1)}, u32[]{:S(2)}, u32[]{:S(2)}) collective-permute-start(bf16[384,384]{1,0:T(8,128)(2,1)} %get-tuple-element.40), channel_id=1, source_target_pairs={{0,8},{1,9},{2,10},{3,11},{4,12},{5,13},{6,14},{7,15},{8,0},{9,1},... | collective-permute-start | bytes 884744 | tf_op jit(solution)/shard_map/ppermute | solution.py:128
  35.4 22.7 %collective-permute-start.10 = (bf16[384,384]{1,0:T(8,128)(2,1)S(1)}, bf16[384,384]{1,0:T(8,128)(2,1)S(1)}, u32[]{:S(2)}, u32[]{:S(2)}) collective-permute-start(bf16[384,384]{1,0:T(8,128)(2,1)S(1)} %collective-permute-done.refs_0_), channel_id=1, source_target_pairs={{0,1},{1,0},{2,3},{3,2},{4,5},{5,4},{6,7},{7,6},{8,9},{9,8},{10,11... | collective-permute-start | bytes 884744 | tf_op jit(solution)/shard_map/ppermute | solution.py:128
  35.7 22.5 %collective-permute-start.6 = (bf16[384,384]{1,0:T(8,128)(2,1)S(1)}, bf16[384,384]{1,0:T(8,128)(2,1)S(1)}, u32[]{:S(2)}, u32[]{:S(2)}) collective-permute-start(bf16[384,384]{1,0:T(8,128)(2,1)S(1)} %collective-permute-done.1.refs_0_), channel_id=1, source_target_pairs={{0,2},{1,3},{2,0},{3,1},{4,6},{5,7},{6,4},{7,5},{8,10},{9,11},{10,... | collective-permute-start | bytes 884744 | tf_op jit(solution)/shard_map/ppermute | solution.py:128
  37.2 34.7 %collective-permute-start.7 = (bf16[384,384]{1,0:T(8,128)(2,1)S(1)}, bf16[384,384]{1,0:T(8,128)(2,1)S(1)}, u32[]{:S(2)}, u32[]{:S(2)}) collective-permute-start(bf16[384,384]{1,0:T(8,128)(2,1)S(1)} %collective-permute-done.1.refs_0_), channel_id=1, source_target_pairs={{0,1},{1,0},{2,3},{3,2},{4,5},{5,4},{6,7},{7,6},{8,9},{9,8},{10,11... | collective-permute-start | bytes 884744 | tf_op jit(solution)/shard_map/ppermute | solution.py:128
  42.6 16.2 %collective-permute-start.11 = (bf16[384,384]{1,0:T(8,128)(2,1)S(1)}, bf16[384,384]{1,0:T(8,128)(2,1)S(1)}, u32[]{:S(2)}, u32[]{:S(2)}) collective-permute-start(bf16[384,384]{1,0:T(8,128)(2,1)S(1)} %collective-permute-done.9.refs_1_), channel_id=1, source_target_pairs={{0,1},{1,0},{2,3},{3,2},{4,5},{5,4},{6,7},{7,6},{8,9},{9,8},{10,11... | collective-permute-start | bytes 884744 | tf_op jit(solution)/shard_map/ppermute | solution.py:128
  58.1 27.1 %collective-permute-start.4 = (bf16[384,384]{1,0:T(8,128)(2,1)S(1)}, bf16[384,384]{1,0:T(8,128)(2,1)S(1)}, u32[]{:S(2)}, u32[]{:S(2)}) collective-permute-start(bf16[384,384]{1,0:T(8,128)(2,1)S(1)} %collective-permute-done.2.refs_0_), channel_id=1, source_target_pairs={{0,1},{1,0},{2,3},{3,2},{4,5},{5,4},{6,7},{7,6},{8,9},{9,8},{10,11... | collective-permute-start | bytes 884744 | tf_op jit(solution)/shard_map/ppermute | solution.py:128
  58.2 13.7 %collective-permute-start.8 = (bf16[384,384]{1,0:T(8,128)(2,1)S(1)}, bf16[384,384]{1,0:T(8,128)(2,1)S(1)}, u32[]{:S(2)}, u32[]{:S(2)}) collective-permute-start(bf16[384,384]{1,0:T(8,128)(2,1)S(1)} %collective-permute-done.6.refs_1_), channel_id=1, source_target_pairs={{0,1},{1,0},{2,3},{3,2},{4,5},{5,4},{6,7},{7,6},{8,9},{9,8},{10,11... | collective-permute-start | bytes 884744 | tf_op jit(solution)/shard_map/ppermute | solution.py:128
  58.7 26.5 %collective-permute-start.5 = (bf16[384,384]{1,0:T(8,128)(2,1)S(1)}, bf16[384,384]{1,0:T(8,128)(2,1)S(1)}, u32[]{:S(2)}, u32[]{:S(2)}) collective-permute-start(bf16[384,384]{1,0:T(8,128)(2,1)S(1)} %collective-permute-done.3.refs_1_), channel_id=1, source_target_pairs={{0,1},{1,0},{2,3},{3,2},{4,5},{5,4},{6,7},{7,6},{8,9},{9,8},{10,11... | collective-permute-start | bytes 884744 | tf_op jit(solution)/shard_map/ppermute | solution.py:128
  113.9 17.8 %collective-permute-start.32 = (bf16[384,384]{1,0:T(8,128)(2,1)S(1)}, bf16[384,384]{1,0:T(8,128)(2,1)S(1)}, u32[]{:S(2)}, u32[]{:S(2)}) collective-permute-start(bf16[384,384]{1,0:T(8,128)(2,1)S(1)} %copy-done.45), channel_id=1, source_target_pairs={{0,1},{1,0},{2,3},{3,2},{4,5},{5,4},{6,7},{7,6},{8,9},{9,8},{10,11... | collective-permute-start | bytes 884744 | tf_op jit(solution)/shard_map/ppermute | solution.py:128
  131.7 20.4 %collective-permute-start.23 = (bf16[384,384]{1,0:T(8,128)(2,1)S(1)}, bf16[384,384]{1,0:T(8,128)(2,1)S(1)}, u32[]{:S(2)}, u32[]{:S(2)}) collective-permute-start(bf16[384,384]{1,0:T(8,128)(2,1)S(1)} %copy-done.40), channel_id=1, source_target_pairs={{0,1},{1,0},{2,3},{3,2},{4,5},{5,4},{6,7},{7,6},{8,9},{9,8},{10,11... | collective-permute-start | bytes 884744 | tf_op jit(solution)/shard_map/ppermute | solution.py:128
  134.8 14.5 %collective-permute-start.29 = (bf16[384,384]{1,0:T(8,128)(2,1)S(1)}, bf16[384,384]{1,0:T(8,128)(2,1)S(1)}, u32[]{:S(2)}, u32[]{:S(2)}) collective-permute-start(bf16[384,384]{1,0:T(8,128)(2,1)S(1)} %add_convert_fusion.3), channel_id=1, source_target_pairs={{0,2},{1,3},{2,0},{3,1},{4,6},{5,7},{6,4},{7,5},{8,10},{9,11},{10,... | collective-permute-start | bytes 884744 | tf_op jit(solution)/shard_map/ppermute | solution.py:128
  136.9 20.6 %collective-permute-start.20 = (bf16[384,384]{1,0:T(8,128)(2,1)}, bf16[384,384]{1,0:T(8,128)(2,1)S(1)}, u32[]{:S(2)}, u32[]{:S(2)}) collective-permute-start(bf16[384,384]{1,0:T(8,128)(2,1)} %get-tuple-element.49), channel_id=1, source_target_pairs={{0,1},{1,0},{2,3},{3,2},{4,5},{5,4},{6,7},{7,6},{8,9},{9,8},{10,11... | collective-permute-start | bytes 884744 | tf_op jit(solution)/shard_map/ppermute | solution.py:128
  144.7 16.8 %collective-permute-start.22 = (bf16[384,384]{1,0:T(8,128)(2,1)S(1)}, bf16[384,384]{1,0:T(8,128)(2,1)S(1)}, u32[]{:S(2)}, u32[]{:S(2)}) collective-permute-start(bf16[384,384]{1,0:T(8,128)(2,1)S(1)} %add_convert_fusion.7), channel_id=1, source_target_pairs={{0,2},{1,3},{2,0},{3,1},{4,6},{5,7},{6,4},{7,5},{8,10},{9,11},{10,... | collective-permute-start | bytes 884744 | tf_op jit(solution)/shard_map/ppermute | solution.py:128
  152.1 23.6 %collective-permute-start.30 = (bf16[384,384]{1,0:T(8,128)(2,1)S(1)}, bf16[384,384]{1,0:T(8,128)(2,1)S(1)}, u32[]{:S(2)}, u32[]{:S(2)}) collective-permute-start(bf16[384,384]{1,0:T(8,128)(2,1)S(1)} %add_convert_fusion.2), channel_id=1, source_target_pairs={{0,8},{1,9},{2,10},{3,11},{4,12},{5,13},{6,14},{7,15},{8,0},{9,1},... | collective-permute-start | bytes 884744 | tf_op jit(solution)/shard_map/ppermute | solution.py:128
  155.8 19.9 %collective-permute-start.26 = (bf16[384,384]{1,0:T(8,128)(2,1)S(1)}, bf16[384,384]{1,0:T(8,128)(2,1)S(1)}, u32[]{:S(2)}, u32[]{:S(2)}) collective-permute-start(bf16[384,384]{1,0:T(8,128)(2,1)S(1)} %add_convert_fusion.4), channel_id=1, source_target_pairs={{0,4},{1,5},{2,6},{3,7},{4,8},{5,9},{6,10},{7,11},{8,12},{9,13},{1... | collective-permute-start | bytes 884744 | tf_op jit(solution)/shard_map/ppermute | solution.py:128
  180.0 14.1 %collective-permute-start.35 = (bf16[512,384]{1,0:T(8,128)(2,1)}, bf16[512,384]{1,0:T(8,128)(2,1)S(1)}, u32[]{:S(2)}, u32[]{:S(2)}) collective-permute-start(bf16[512,384]{1,0:T(8,128)(2,1)} %get-tuple-element.65.refs_0_), channel_id=1, source_target_pairs={{0,4},{1,5},{2,6},{3,7},{4,8},{5,9},{6,10},{7,11},{8,12},{9,13},{1... | collective-permute-start | bytes 1179656 | tf_op jit(solution)/shard_map/ppermute | solution.py:128
  181.4 18.1 %collective-permute-start.36 = (bf16[512,384]{1,0:T(8,128)(2,1)}, bf16[512,384]{1,0:T(8,128)(2,1)S(1)}, u32[]{:S(2)}, u32[]{:S(2)}) collective-permute-start(bf16[512,384]{1,0:T(8,128)(2,1)} %get-tuple-element.65.refs_0_), channel_id=1, source_target_pairs={{0,12},{1,13},{2,14},{3,15},{4,0},{5,1},{6,2},{7,3},{8,4},{9,5},{1... | collective-permute-start | bytes 1179656 | tf_op jit(solution)/shard_map/ppermute | solution.py:128
  183.9 43.4 %collective-permute-start.47 = (bf16[512,384]{1,0:T(8,128)(2,1)}, bf16[512,384]{1,0:T(8,128)(2,1)S(1)}, u32[]{:S(2)}, u32[]{:S(2)}) collective-permute-start(bf16[512,384]{1,0:T(8,128)(2,1)} %get-tuple-element.65.refs_0_), channel_id=1, source_target_pairs={{0,2},{1,3},{2,0},{3,1},{4,6},{5,7},{6,4},{7,5},{8,10},{9,11},{10,... | collective-permute-start | bytes 1179656 | tf_op jit(solution)/shard_map/ppermute | solution.py:128
  185.4 42.8 %collective-permute-start.48 = (bf16[512,384]{1,0:T(8,128)(2,1)}, bf16[512,384]{1,0:T(8,128)(2,1)S(1)}, u32[]{:S(2)}, u32[]{:S(2)}) collective-permute-start(bf16[512,384]{1,0:T(8,128)(2,1)} %get-tuple-element.65.refs_0_), channel_id=1, source_target_pairs={{0,1},{1,0},{2,3},{3,2},{4,5},{5,4},{6,7},{7,6},{8,9},{9,8},{10,11... | collective-permute-start | bytes 1179656 | tf_op jit(solution)/shard_map/ppermute | solution.py:128
  199.6 29.1 %collective-permute-start.44 = (bf16[512,384]{1,0:T(8,128)(2,1)S(1)}, bf16[512,384]{1,0:T(8,128)(2,1)S(1)}, u32[]{:S(2)}, u32[]{:S(2)}) collective-permute-start(bf16[512,384]{1,0:T(8,128)(2,1)S(1)} %collective-permute-done.35.refs_0_), channel_id=1, source_target_pairs={{0,2},{1,3},{2,0},{3,1},{4,6},{5,7},{6,4},{7,5},{8,10},{9,11},{10,... | collective-permute-start | bytes 1179656 | tf_op jit(solution)/shard_map/ppermute | solution.py:128
  201.1 27.6 %collective-permute-start.37 = (bf16[512,384]{1,0:T(8,128)(2,1)}, bf16[512,384]{1,0:T(8,128)(2,1)S(1)}, u32[]{:S(2)}, u32[]{:S(2)}) collective-permute-start(bf16[512,384]{1,0:T(8,128)(2,1)} %get-tuple-element.65.refs_0_), channel_id=1, source_target_pairs={{0,8},{1,9},{2,10},{3,11},{4,12},{5,13},{6,14},{7,15},{8,0},{9,1},... | collective-permute-start | bytes 1179656 | tf_op jit(solution)/shard_map/ppermute | solution.py:128
  228.1 18.9 %collective-permute-start.45 = (bf16[512,384]{1,0:T(8,128)(2,1)S(1)}, bf16[512,384]{1,0:T(8,128)(2,1)S(1)}, u32[]{:S(2)}, u32[]{:S(2)}) collective-permute-start(bf16[512,384]{1,0:T(8,128)(2,1)S(1)} %collective-permute-done.35.refs_0_), channel_id=1, source_target_pairs={{0,1},{1,0},{2,3},{3,2},{4,5},{5,4},{6,7},{7,6},{8,9},{9,8},{10,11... | collective-permute-start | bytes 1179656 | tf_op jit(solution)/shard_map/ppermute | solution.py:128
  228.7 19.1 %collective-permute-start.46 = (bf16[512,384]{1,0:T(8,128)(2,1)S(1)}, bf16[512,384]{1,0:T(8,128)(2,1)}, u32[]{:S(2)}, u32[]{:S(2)}) collective-permute-start(bf16[512,384]{1,0:T(8,128)(2,1)S(1)} %collective-permute-done.44.refs_1_), channel_id=1, source_target_pairs={{0,1},{1,0},{2,3},{3,2},{4,5},{5,4},{6,7},{7,6},{8,9},{9,8},{10,11... | collective-permute-start | bytes 1179656 | tf_op jit(solution)/shard_map/ppermute | solution.py:128
  228.7 18.9 %collective-permute-start.38 = (bf16[512,384]{1,0:T(8,128)(2,1)S(1)}, bf16[512,384]{1,0:T(8,128)(2,1)S(1)}, u32[]{:S(2)}, u32[]{:S(2)}) collective-permute-start(bf16[512,384]{1,0:T(8,128)(2,1)S(1)} %collective-permute-done.37.refs_0_), channel_id=1, source_target_pairs={{0,2},{1,3},{2,0},{3,1},{4,6},{5,7},{6,4},{7,5},{8,10},{9,11},{10,... | collective-permute-start | bytes 1179656 | tf_op jit(solution)/shard_map/ppermute | solution.py:128
  231.8 25.5 %collective-permute-start.42 = (bf16[512,384]{1,0:T(8,128)(2,1)S(1)}, bf16[512,384]{1,0:T(8,128)(2,1)S(1)}, u32[]{:S(2)}, u32[]{:S(2)}) collective-permute-start(bf16[512,384]{1,0:T(8,128)(2,1)S(1)} %collective-permute-done.36.refs_0_), channel_id=1, source_target_pairs={{0,1},{1,0},{2,3},{3,2},{4,5},{5,4},{6,7},{7,6},{8,9},{9,8},{10,11... | collective-permute-start | bytes 1179656 | tf_op jit(solution)/shard_map/ppermute | solution.py:128
  238.4 19.0 %collective-permute-start.43 = (bf16[512,384]{1,0:T(8,128)(2,1)S(1)}, bf16[512,384]{1,0:T(8,128)(2,1)S(1)}, u32[]{:S(2)}, u32[]{:S(2)}) collective-permute-start(bf16[512,384]{1,0:T(8,128)(2,1)S(1)} %collective-permute-done.41.refs_1_), channel_id=1, source_target_pairs={{0,1},{1,0},{2,3},{3,2},{4,5},{5,4},{6,7},{7,6},{8,9},{9,8},{10,11... | collective-permute-start | bytes 1179656 | tf_op jit(solution)/shard_map/ppermute | solution.py:128
  247.1 21.3 %collective-permute-start.39 = (bf16[512,384]{1,0:T(8,128)(2,1)S(1)}, bf16[512,384]{1,0:T(8,128)(2,1)S(1)}, u32[]{:S(2)}, u32[]{:S(2)}) collective-permute-start(bf16[512,384]{1,0:T(8,128)(2,1)S(1)} %collective-permute-done.37.refs_0_), channel_id=1, source_target_pairs={{0,1},{1,0},{2,3},{3,2},{4,5},{5,4},{6,7},{7,6},{8,9},{9,8},{10,11... | collective-permute-start | bytes 1179656 | tf_op jit(solution)/shard_map/ppermute | solution.py:128
  247.6 20.7 %collective-permute-start.40 = (bf16[512,384]{1,0:T(8,128)(2,1)S(1)}, bf16[512,384]{1,0:T(8,128)(2,1)S(1)}, u32[]{:S(2)}, u32[]{:S(2)}) collective-permute-start(bf16[512,384]{1,0:T(8,128)(2,1)S(1)} %collective-permute-done.38.refs_1_), channel_id=1, source_target_pairs={{0,1},{1,0},{2,3},{3,2},{4,5},{5,4},{6,7},{7,6},{8,9},{9,8},{10,11... | collective-permute-start | bytes 1179656 | tf_op jit(solution)/shard_map/ppermute | solution.py:128
  293.8 19.5 %collective-permute-start.58 = (f32[3,512]{0,1:T(8,128)S(1)}, f32[3,512]{0,1:T(8,128)S(1)}, u32[]{:S(2)}, u32[]{:S(2)}) collective-permute-start(f32[3,512]{0,1:T(8,128)S(1)} %pad_maximum_fusion.1), channel_id=1, source_target_pairs={{0,8},{1,9},{2,10},{3,11},{4,12},{5,13},{6,14},{7,15},{8,0},{9,1},... | collective-permute-start | bytes 18440 | tf_op jit(solution)/shard_map/ppermute | solution.py:128
  295.7 17.6 %collective-permute-start.59 = (f32[3,512]{0,1:T(8,128)S(1)}, f32[3,512]{0,1:T(8,128)S(1)}, u32[]{:S(2)}, u32[]{:S(2)}) collective-permute-start(f32[3,512]{0,1:T(8,128)S(1)} %pad_maximum_fusion.1), channel_id=1, source_target_pairs={{0,12},{1,13},{2,14},{3,15},{4,0},{5,1},{6,2},{7,3},{8,4},{9,5},{1... | collective-permute-start | bytes 18440 | tf_op jit(solution)/shard_map/ppermute | solution.py:128
  (74 other events, 841.0 us)

commit v3 on v2

--- a/solution.py
+++ b/solution.py
@@ -121,7 +121,8 @@
     return jnp.where(in_length, own_rows, jnp.zeros_like(own_rows)).astype(jnp.float32)
 
 VMEM_BYTES = 56 * 1024 * 1024
-ORDER = (0, 1, 3, 2)
+GROUPS = ((0,), (1, 3), (2,))
+TIERS = ((256, 192), (288, 224), (320, 256), (384, 288))
 
 
 def send(array, pairs):
@@ -138,6 +139,10 @@
 
 def plane_pairs(k):
     return [(i, ((i >> 2) + k) % 4 * 4 + (i & 3)) for i in range(16)]
+
+
+def after(value, *others):
+    return lax.optimization_barrier((value, *others))[0]
 
 
 def summed_all(array):
@@ -190,15 +195,27 @@
     )(slot_rows, x, gain)
 
 
-def place(where_ref, blocks, wide_ref):
-    cols = blocks[0].shape[1]
-    for b, block in enumerate(blocks):
-        at = pl.multiple_of(where_ref[1 + b] * cols, 128)
-        wide_ref[:, pl.ds(at, cols)] = block[...]
-
-
-def hidden_kernel(first, last, where_ref, *refs):
-    blocks, (wg, wu), refs = refs[:4], refs[4:6], refs[6:]
+def place(where_ref, chunk, blocks, wide_ref):
+    rows, cols = wide_ref.shape[0], blocks[0].shape[1]
+    for g in range(chunk):
+        for b, block in enumerate(blocks):
+            at = pl.multiple_of(g * 4 * cols + where_ref[b] * cols, 128)
+            wide_ref[:, pl.ds(at, cols)] = block[g * rows : (g + 1) * rows, :]
+
+
+def product(wide, weights):
+    depth = weights[0].shape[0]
+    value = None
+    for g, w in enumerate(weights):
+        part = jnp.dot(
+            wide[:, g * depth : (g + 1) * depth], w[...], preferred_element_type=jnp.float32
+        )
+        value = part if value is None else value + part
+    return value
+
+
+def hidden_kernel(chunk, first, last, where_ref, *refs):
+    blocks, wg, wu, refs = refs[:4], refs[4 : 4 + chunk], refs[4 + chunk : 4 + 2 * chunk], refs[4 + 2 * chunk :]
     if not first:
         g_in, u_in, refs = refs[0], refs[1], refs[2:]
     if last:
@@ -208,10 +225,10 @@
 
     @pl.when(pl.program_id(0) == 0)
     def _():
-        place(where_ref, blocks, wide)
-
-    g = jnp.dot(wide[...], wg[...], preferred_element_type=jnp.float32)
-    u = jnp.dot(wide[...], wu[...], preferred_element_type=jnp.float32)
+        place(where_ref, chunk, blocks, wide)
+
+    g = product(wide, wg)
+    u = product(wide, wu)
     if not first:
         g = g + g_in[...]
         u = u + u_in[...]
@@ -224,45 +241,53 @@
         u_out[...] = u
 
 
-def hidden_part(where, blocks, w_gate, w_up, sums, inv):
-    rows, cols = blocks[0].shape
+def weight_specs(chunk, depth, tile):
+    return [
+        pl.BlockSpec((depth, tile), functools.partial(lambda g, n, w: (w[4 + g], n), g))
+        for g in range(chunk)
+    ]
+
+
+def hidden_part(where, blocks, slots, w_gate, w_up, sums, inv):
+    cols = blocks[0].shape[1]
+    chunk = blocks[0].shape[0] // slots
     width = w_gate.shape[1]
     tile = 512
     first, last = sums is None, inv is not None
-    whole = pl.BlockSpec((rows, cols), lambda n, w: (0, 0))
-    weight = pl.BlockSpec((4 * cols, tile), lambda n, w: (w[0], n))
-    out_tile = pl.BlockSpec((rows, tile), lambda n, w: (0, n))
-    ins, specs = [where, *blocks, w_gate, w_up], [whole] * 4 + [weight] * 2
+    whole = pl.BlockSpec((chunk * slots, cols), lambda n, w: (0, 0))
+    out_tile = pl.BlockSpec((slots, tile), lambda n, w: (0, n))
+    ins = [where, *blocks] + [w_gate] * chunk + [w_up] * chunk
+    specs = [whole] * 4 + weight_specs(chunk, 4 * cols, tile) * 2
     aliases = {}
     if not first:
+        if not last:
+            aliases = {len(ins): 0, len(ins) + 1: 1}
         ins += list(sums)
         specs += [out_tile] * 2
-        if not last:
-            aliases = {7: 0, 8: 1}
     if last:
         ins.append(inv)
-        specs.append(pl.BlockSpec((rows, 1), lambda n, w: (0, 0)))
-        outs, out_specs = jax.ShapeDtypeStruct((rows, width), jnp.bfloat16), out_tile
+        specs.append(pl.BlockSpec((slots, 1), lambda n, w: (0, 0)))
+        outs, out_specs = jax.ShapeDtypeStruct((slots, width), jnp.bfloat16), out_tile
     else:
-        outs = [jax.ShapeDtypeStruct((rows, width), jnp.float32)] * 2
+        outs = [jax.ShapeDtypeStruct((slots, width), jnp.float32)] * 2
         out_specs = [out_tile] * 2
     return pl.pallas_call(
-        functools.partial(hidden_kernel, first, last),
+        functools.partial(hidden_kernel, chunk, first, last),
         out_shape=outs,
         grid_spec=pltpu.PrefetchScalarGridSpec(
             num_scalar_prefetch=1,
             grid=(width // tile,),
             in_specs=specs,
             out_specs=out_specs,
-            scratch_shapes=[pltpu.VMEM((rows, 4 * cols), jnp.bfloat16)],
+            scratch_shapes=[pltpu.VMEM((slots, chunk * 4 * cols), jnp.bfloat16)],
         ),
         input_output_aliases=aliases,
         compiler_params=params(1),
-        cost_estimate=cost(rows, 4 * cols, 2 * width, 16 * rows * width),
+        cost_estimate=cost(slots, chunk * 4 * cols, 2 * width, 16 * slots * width),
     )(*ins)
 
 
-def down_kernel(where_ref, h_ref, w_ref, gate_ref, o_own, o_row, o_core, o_far, total):
+def down_kernel(where_ref, h_ref, w_ref, gate_ref, o_own, o_row, o_core, total):
     @pl.when(pl.program_id(0) == 0)
     def _():
         total[...] = jnp.zeros_like(total)
@@ -271,29 +296,36 @@
 
     @pl.when(pl.program_id(0) == pl.num_programs(0) - 1)
     def _():
-        cols = o_own.shape[1]
-        for b, out in enumerate((o_own, o_row, o_core, o_far)):
-            at = pl.multiple_of(where_ref[1 + b] * cols, 128)
-            out[...] = (total[:, pl.ds(at, cols)] * gate_ref[...]).astype(out.dtype)
+        rows, cols = o_own.shape
+        for b in range(4):
+            at = pl.multiple_of(where_ref[b] * cols, 128)
+            value = total[:, pl.ds(at, cols)] * gate_ref[...]
+            if b < 2:
+                (o_own, o_row)[b][...] = value
+            else:
+                o_core[(b - 2) * rows : (b - 1) * rows, :] = value.astype(jnp.bfloat16)
 
 
 def down_part(where, hidden, w_down, gate_slot, cols):
     rows, inner = hidden.shape
-    depth = 512
+    depth = 1024
     block = pl.BlockSpec((rows, cols), lambda j, w: (0, 0))
-    kinds = (jnp.float32, jnp.float32, jnp.bfloat16, jnp.bfloat16)
     return pl.pallas_call(
         down_kernel,
-        out_shape=[jax.ShapeDtypeStruct((rows, cols), kind) for kind in kinds],
+        out_shape=[
+            jax.ShapeDtypeStruct((rows, cols), jnp.float32),
+            jax.ShapeDtypeStruct((rows, cols), jnp.float32),
+            jax.ShapeDtypeStruct((2 * rows, cols), jnp.bfloat16),
+        ],
         grid_spec=pltpu.PrefetchScalarGridSpec(
             num_scalar_prefetch=1,
             grid=(inner // depth,),
             in_specs=[
                 pl.BlockSpec((rows, depth), lambda j, w: (0, j)),
-                pl.BlockSpec((depth, 4 * cols), lambda j, w: (j, w[0])),
+                pl.BlockSpec((depth, 4 * cols), lambda j, w: (j, w[4])),
                 pl.BlockSpec((rows, 1), lambda j, w: (0, 0)),
             ],
-            out_specs=[block] * 4,
+            out_specs=[block] * 2 + [pl.BlockSpec((2 * rows, cols), lambda j, w: (0, 0))],
             scratch_shapes=[pltpu.VMEM((rows, 4 * cols), jnp.float32)],
         ),
         compiler_params=params(1),
@@ -327,8 +359,8 @@
     )(slot_cols, x, gain, *parts)
 
 
-def vocab_kernel(first, last, where_ref, *refs):
-    blocks, w_ref, refs = refs[:4], refs[4], refs[5:]
+def vocab_kernel(chunk, first, last, where_ref, *refs):
+    blocks, weights, refs = refs[:4], refs[4 : 4 + chunk], refs[4 + chunk :]
     if not first:
         sum_in, refs = refs[0], refs[1:]
     if last:
@@ -339,9 +371,9 @@
 
     @pl.when(n == 0)
     def _():
-        place(where_ref, blocks, wide)
-
-    value = jnp.dot(wide[...], w_ref[...], preferred_element_type=jnp.float32)
+        place(where_ref, chunk, blocks, wide)
+
+    value = product(wide, weights)
     if not first:
         value = value + sum_in[...]
     if not last:
@@ -374,22 +406,23 @@
         out[...] = jnp.where(lane == 0, top[...], jnp.where(lane == 1, total[...], picked[...]))
 
 
-def vocab_part(where, blocks, lm_head, sums, inv, local_ids):
-    rows, cols = blocks[0].shape
+def vocab_part(where, blocks, rows, lm_head, sums, inv, local_ids):
+    cols = blocks[0].shape[1]
+    chunk = blocks[0].shape[0] // rows
     width = lm_head.shape[1]
     tile = 512
     first, last = sums is None, inv is not None
-    whole = pl.BlockSpec((rows, cols), lambda n, w: (0, 0))
+    whole = pl.BlockSpec((chunk * rows, cols), lambda n, w: (0, 0))
     out_tile = pl.BlockSpec((rows, tile), lambda n, w: (0, n))
-    ins = [where, *blocks, lm_head]
-    specs = [whole] * 4 + [pl.BlockSpec((4 * cols, tile), lambda n, w: (w[0], n))]
+    ins = [where, *blocks] + [lm_head] * chunk
+    specs = [whole] * 4 + weight_specs(chunk, 4 * cols, tile)
     aliases = {}
     if not first:
+        if not last:
+            aliases = {len(ins): 0}
         ins.append(sums)
         specs.append(out_tile)
-        if not last:
-            aliases = {6: 0}
-    scratch = [pltpu.VMEM((rows, 4 * cols), jnp.bfloat16)]
+    scratch = [pltpu.VMEM((rows, chunk * 4 * cols), jnp.bfloat16)]
     if last:
         ins += [inv, local_ids]
         specs += [pl.BlockSpec((rows, 1), lambda n, w: (0, 0))] * 2
@@ -399,7 +432,7 @@
     else:
         outs, out_specs = jax.ShapeDtypeStruct((rows, width), jnp.float32), out_tile
     return pl.pallas_call(
-        functools.partial(vocab_kernel, first, last),
+        functools.partial(vocab_kernel, chunk, first, last),
         out_shape=outs,
         grid_spec=pltpu.PrefetchScalarGridSpec(
             num_scalar_prefetch=1,
@@ -410,22 +443,110 @@
         ),
         input_output_aliases=aliases,
         compiler_params=params(1),
-        cost_estimate=cost(rows, 4 * cols, width, 8 * rows * width),
+        cost_estimate=cost(rows, chunk * 4 * cols, width, 8 * rows * width),
     )(*ins)
 
 
-def spread(by_offset):
-    arrived = {0: by_offset[0]}
-    arrived[1] = send(by_offset[1], plane_pairs(1))
-    arrived[3] = send(by_offset[3], plane_pairs(3))
-    later, _, _ = lax.optimization_barrier((by_offset[2], arrived[1], arrived[3]))
-    arrived[2] = send(later, plane_pairs(2))
-    chunks = {}
-    for k in ORDER:
-        own = arrived[k]
-        row = send(own, row_pairs())
-        chunks[k] = (own, row, send(own, core_pairs()), send(row, core_pairs()))
-    return chunks
+def shared(own, row):
+    return (own, row, send(own, core_pairs()), send(row, core_pairs()))
+
+
+def spread_and_sum(by_offset, part):
+    a1 = send(by_offset[1], plane_pairs(1))
+    a3 = send(by_offset[3], plane_pairs(3))
+    row0 = send(by_offset[0], row_pairs())
+    a2 = send(after(by_offset[2], a1, a3), plane_pairs(2))
+    near = jnp.concatenate([a1, a3], axis=0)
+    row13 = send(near, row_pairs())
+    sums = part(0, shared(by_offset[0], row0), None)
+    a2 = after(a2, sums)
+    row2 = send(a2, row_pairs())
+    sums = part(1, shared(near, row13), sums)
+    row2 = after(row2, sums)
+    return part(2, shared(a2, row2), sums)
+
+
+def live_part(
+    residual_in,
+    norm_gain,
+    final_gain,
+    w_gate,
+    w_up,
+    w_down,
+    lm_head,
+    target_ids,
+    packed,
+    slot,
+    gate,
+    in_squares,
+    live_rows,
+    slots,
+):
+    tokens, cols = residual_in.shape
+    me = lax.axis_index("tensor")
+    plane, row, core = me // 4, me // 2 % 2, me % 2
+    at = [row * 2 + core, (1 - row) * 2 + core, row * 2 + 1 - core, (1 - row) * 2 + 1 - core]
+    planes = [(plane + k) % 4 for k in range(4)]
+    group_at = [
+        jnp.stack(at + [planes[(4 - k) % 4] for k in group]).astype(jnp.int32) for group in GROUPS
+    ]
+    down_at = [jnp.stack(at + [planes[k]]).astype(jnp.int32) for k in range(4)]
+
+    slot_rows = jnp.concatenate(
+        [slot.T, packed[None, :], jnp.zeros((3, tokens), jnp.int32)], axis=0
+    )
+    *picked_rows, x_live = dispatch(slot_rows, residual_in, norm_gain[None, :], slots, live_rows)
+
+    in_total = summed_all(in_squares)
+    in_scale = 1.0 / jnp.sqrt(in_total / D + epsilon)
+    own_slot = one_hot(slot[:, 0], slots)
+    inv_slot = jnp.sum(jnp.where(own_slot, in_scale[None, :], 0.0), axis=1, keepdims=True)
+    gate_slot = jnp.sum(jnp.where(own_slot, gate[:, 0][None, :], 0.0), axis=1, keepdims=True)
+    live_at = one_hot(packed, live_rows)
+    slot_live = (
+        jnp.sum(jnp.where(live_at[:, :, None], slot[None, :, :] + 1, 0), axis=1) - 1
+    )
+    slot_live = jnp.stack([slot_live[:, (4 - k) % 4] for k in range(4)], axis=1)
+    target_live = jnp.sum(jnp.where(live_at, target_ids[None, :], 0), axis=1, keepdims=True)
+
+    hidden = spread_and_sum(
+        picked_rows,
+        lambda g, blocks, sums: hidden_part(
+            group_at[g], blocks, slots, w_gate, w_up, sums, inv_slot if g == 2 else None
+        ),
+    )
+
+    parts, heard, crossed, own = {}, {}, {}, {}
+    waits = ()
+    for turn, k in enumerate((2, 1, 3, 0)):
+        kept, across, near = down_part(down_at[k], after(hidden, *waits), w_down, gate_slot, cols)
+        heard[turn] = send(near, core_pairs())
+        far = heard[turn][slots:].astype(jnp.float32)
+        crossed[turn] = send((across + far).astype(jnp.bfloat16), row_pairs())
+        total = (
+            kept + heard[turn][:slots].astype(jnp.float32) + crossed[turn].astype(jnp.float32)
+        ).astype(jnp.bfloat16)
+        parts[k] = send(total, plane_pairs(k)) if k else total
+        waits = (kept,)
+        if turn >= 1:
+            waits += (heard[turn - 1],)
+        if turn >= 2:
+            waits += (crossed[turn - 2],)
+
+    scaled, squares = mix(slot_live, x_live, final_gain[None, :], [parts[k] for k in range(4)])
+    out_total = summed_all(squares.reshape(-1))
+    out_scale = (1.0 / jnp.sqrt(out_total / D + epsilon))[:, None]
+    local_ids = target_live - me * lm_head.shape[1]
+    stats = spread_and_sum(
+        [scaled] * 4,
+        lambda g, blocks, sums: vocab_part(
+            group_at[g], blocks, live_rows, lm_head, sums, out_scale if g == 2 else None, local_ids
+        ),
+    )
+    spot = packed[:, None] == jnp.arange(live_rows, dtype=jnp.int32)[None, :]
+    return jnp.stack(
+        [jnp.sum(jnp.where(spot, stats[:, j][None, :], 0.0), axis=1) for j in range(3)]
+    )
 
 
 def fast_body(
@@ -440,16 +561,11 @@
     lm_head,
     target_ids,
     lengths,
-    live_rows,
-    slots,
 ):
-    tokens, cols = residual_in.shape
+    tokens = residual_in.shape[0]
+    devices = lax.axis_size("tensor")
     me = lax.axis_index("tensor")
-    plane, row, core = me // 4, me // 2 % 2, me % 2
-    offsets = [row * 2 + core, (1 - row) * 2 + core, row * 2 + 1 - core, (1 - row) * 2 + 1 - core]
-    where = {k: jnp.stack([(plane + k) % 4, *offsets]).astype(jnp.int32) for k in range(4)}
-
-    place_in = jnp.arange(tokens, dtype=jnp.int32)
+    plane = me // 4
     cands = lengths.shape[0]
     cand = jnp.arange(cands, dtype=jnp.int32)
     starts = jnp.sum(jnp.where(cand[None, :] < cand[:, None], lengths[None, :], 0), axis=1)
@@ -460,83 +576,55 @@
     expert_at = (plane + jnp.arange(EXPERTS, dtype=jnp.int32)) % EXPERTS
     hit = (expert_ids[:, :, None] == expert_at[None, None, :]) & live[:, None, None]
     used = jnp.any(hit, axis=1)
+    fullest = jnp.max(jnp.sum(used.astype(jnp.int32), axis=0))
+    alive = jnp.sum(lengths)
+    need = jnp.zeros((), jnp.float32)
+    for rows, slots in TIERS:
+        need = need + jnp.where((alive > rows) | (fullest > slots), 1.0, 0.0)
+    pairs = [(g, g ^ 1) for g in range(2)]
+    need = jnp.maximum(need, lax.ppermute(need, "groups", pairs))
+
     gate = jnp.sum(jnp.where(hit, gate_values[:, :, None], 0.0), axis=1)
+    place_in = jnp.arange(tokens, dtype=jnp.int32)
     earlier = (place_in[None, :] < place_in[:, None]).astype(jnp.bfloat16)
     rank = jnp.dot(earlier, used.astype(jnp.bfloat16), preferred_element_type=jnp.float32)
     slot = jnp.where(used, rank.astype(jnp.int32), -1)
-
-    slot_rows = jnp.concatenate(
-        [slot.T, packed[None, :], jnp.zeros((3, tokens), jnp.int32)], axis=0
-    )
-    *picked_rows, x_live = dispatch(slot_rows, residual_in, norm_gain[None, :], slots, live_rows)
-    chunks = spread(picked_rows)
-
     stream = residual_in.astype(jnp.float32)
-    in_total = summed_all(jnp.sum(stream * stream, axis=1))
-    in_scale = 1.0 / jnp.sqrt(in_total / D + epsilon)
-    own_slot = one_hot(slot[:, 0], slots)
-    inv_slot = jnp.sum(jnp.where(own_slot, in_scale[None, :], 0.0), axis=1, keepdims=True)
-    gate_slot = jnp.sum(jnp.where(own_slot, gate[:, 0][None, :], 0.0), axis=1, keepdims=True)
-    live_at = one_hot(packed, live_rows)
-    slot_live = (
-        jnp.sum(jnp.where(live_at[:, :, None], slot[None, :, :] + 1, 0), axis=1) - 1
-    )
-    slot_live = jnp.stack([slot_live[:, (4 - k) % 4] for k in range(4)], axis=1)
-    target_live = jnp.sum(jnp.where(live_at, target_ids[None, :], 0), axis=1, keepdims=True)
-
-    sums = None
-    for k in ORDER:
-        last = k == ORDER[-1]
-        sums = hidden_part(
-            where[(4 - k) % 4], chunks[k], w_gate, w_up, sums, inv_slot if last else None
-        )
-    hidden = sums
-
-    parts = {}
-    for k in (2, 1, 3, 0):
-        own, across, near, far = down_part(where[k], hidden, w_down, gate_slot, cols)
-        near = send(near, core_pairs())
-        far = send(far, core_pairs())
-        across = send((across + far.astype(jnp.float32)).astype(jnp.bfloat16), row_pairs())
-        own = own + near.astype(jnp.float32) + across.astype(jnp.float32)
-        own = own.astype(jnp.bfloat16)
-        parts[k] = send(own, plane_pairs(k)) if k else own
-
-    scaled, squares = mix(slot_live, x_live, final_gain[None, :], [parts[k] for k in range(4)])
-    chunks = spread([scaled] * 4)
-    out_total = summed_all(squares.reshape(-1))
-    out_scale = (1.0 / jnp.sqrt(out_total / D + epsilon))[:, None]
-    local_ids = target_live - me * lm_head.shape[1]
-    sums = None
-    for k in ORDER:
-        last = k == ORDER[-1]
-        sums = vocab_part(
-            where[(4 - k) % 4], chunks[k], lm_head, sums, out_scale if last else None, local_ids
-        )
-    stats = sums[:, :3].T
-
-    def joined(a, b):
-        top = jnp.maximum(a[0], b[0])
-        return jnp.stack(
-            [top, a[1] * jnp.exp(a[0] - top) + b[1] * jnp.exp(b[0] - top), a[2] + b[2]]
-        )
-
-    stats = joined(stats, send(stats, core_pairs()))
-    stats = joined(stats, send(stats, row_pairs()))
-    others = [send(stats, plane_pairs(k)) for k in (1, 2, 3)]
-    stats = joined(joined(stats, others[0]), joined(others[1], others[2]))
-    logprob = stats[2] - stats[0] - jnp.log(stats[1])
-    rows_dev = tokens // lax.axis_size("tensor")
-    own_packed = lax.dynamic_slice_in_dim(packed, me * rows_dev, rows_dev)
-    mine = own_packed[:, None] == jnp.arange(live_rows, dtype=jnp.int32)[None, :]
-    return jnp.sum(jnp.where(mine, logprob[None, :], 0.0), axis=1)
+    in_squares = jnp.sum(stream * stream, axis=1)
+
+    stats = lax.switch(
+        need.astype(jnp.int32),
+        [
+            functools.partial(live_part, live_rows=rows, slots=slots)
+            for rows, slots in TIERS + ((tokens, CAP),)
+        ],
+        residual_in,
+        norm_gain,
+        final_gain,
+        w_gate,
+        w_up,
+        w_down,
+        lm_head,
+        target_ids,
+        packed,
+        slot,
+        gate,
+        in_squares,
+    )
+    rows_dev = tokens // devices
+    stats = stats.reshape(3, devices, rows_dev).transpose(1, 0, 2)
+    stats = lax.all_to_all(stats, "tensor", 0, 0, tiled=True)
+    top = jnp.max(stats[:, 0], axis=0)
+    total = jnp.sum(stats[:, 1] * jnp.exp(stats[:, 0] - top[None, :]), axis=0)
+    logprob = jnp.sum(stats[:, 2], axis=0) - top - jnp.log(total)
+    own_live = lax.dynamic_slice_in_dim(packed, me * rows_dev, rows_dev) >= 0
+    return jnp.where(own_live, logprob, 0.0)
 
 
 def body(*args):
-    if lax.axis_size("tensor") != 16:
-        return plain_body(*args)
-    tokens = args[0].shape[0]
-    return fast_body(*args, live_rows=tokens, slots=CAP)
+    if lax.axis_size("tensor") == 16 and lax.axis_size("groups") == 2:
+        return fast_body(*args)
+    return plain_body(*args)
 
 
 def solution(mesh):

time: 319 us -> 262 us (0.82)
  waiting for transfers between devices: 105 us -> 68.7 us
  Pallas kernels: 124 us -> 92.6 us
  loops' own time: 0 us -> 16.2 us
  starting transfers between devices: 55.1 us -> 44.8 us
  between operations: 0.66 us -> 6.24 us
    ppermute x60 -> x45, waiting for transfers between devices: 105 us -> 62.1 us  [send(): return lax.ppermute(array, 'tensor', pairs)]
    pallas_call x8 -> x6, Pallas kernels: 85.1 us -> 62.4 us  [the longest x3 35.7 us: hidden_part(): pl.pallas_call(functools.partial(hidden_kernel, chunk, first, last), out_...]
    ppermute x60 -> x45, starting transfers between devices: 55.1 us -> 36.6 us  [send(): return lax.ppermute(array, 'tensor', pairs)]
    another operation x0 -> x1, loops' own time: none -> 16.2 us  [fast_body(): lax.switch(need.astype(jnp.int32), [functools.partial(live_part, live_row...]
    pallas_call x4, Pallas kernels: 32 us -> 24.9 us  [down_part(): pl.pallas_call(down_kernel, out_shape=[jax.ShapeDtypeStruct((rows, cols),...]
    all_to_all x0 -> x1, waiting for transfers between devices: none -> 6.63 us  [fast_body(): stats = lax.all_to_all(stats, 'tensor', 0, 0, tiled=True)]
    unnamed x92 -> x0, local copies, waits for them, and re-layouts: 6.42 us -> none
    cond x0 -> x70, local copies, waits for them, and re-layouts: none -> 5.13 us
  transfers between devices with their start and end apart: 60 -> 47, of which waited for: 21 -> 17; matrix products, arithmetic and copies ran while one was open for 5% -> 6% of each run, Pallas kernels for 25% -> 24%
where the time goes in v3:
time: 262 us; the launch traced here: 258 us
  Pallas kernels  92.6 us (35%)
  waiting for transfers between devices  68.7 us (26%)
  starting transfers between devices  44.8 us (17%)
  local copies, waits for them, and re-layouts  16.5 us (6%)
  loops' own time  16.2 us (6%)
  other arithmetic  12.2 us (5%)
  between operations  6.24 us (2%)
    ppermute x45, waiting for transfers between devices, send(): return lax.ppermute(array, 'tensor', pairs)  62.1 us
    ppermute x45, starting transfers between devices, send(): return lax.ppermute(array, 'tensor', pairs)  36.6 us
    pallas_call x3, Pallas kernels, hidden_part(): pl.pallas_call(functools.partial(hidden_kernel, chunk, first, last), out_...  35.7 us
    pallas_call x3, Pallas kernels, vocab_part(): pl.pallas_call(functools.partial(vocab_kernel, chunk, first, last), out_s...  26.7 us
    pallas_call x4, Pallas kernels, down_part(): pl.pallas_call(down_kernel, out_shape=[jax.ShapeDtypeStruct((rows, cols),...  24.9 us
    another operation x1, loops' own time, fast_body(): lax.switch(need.astype(jnp.int32), [functools.partial(live_part, live_row...  16.2 us
    all_to_all x1, waiting for transfers between devices, fast_body(): stats = lax.all_to_all(stats, 'tensor', 0, 0, tiled=True)  6.63 us
  transfers between devices with their start and end apart: 47, of which 17 were waited for; matrix products, arithmetic and copies ran while one was open for 6% of the time, Pallas kernels for 24%

profile of v3, /device:TPU:0, one launch (start us, length us, event | category | flops | bytes accessed | tf_op | source)
XLA Modules:
  0.0 257.6 jit_solution(14738326412550607677)
XLA Ops:
  8.7 4.3 %collective-permute-start.225 = (f32[]{:T(128)}, f32[]{:T(128)}, u32[]{:S(2)}, u32[]{:S(2)}) collective-permute-start(f32[]{:T(128)} %add.648), channel_id=1, source_target_pairs={{0,16},{16,0},{1,17},{17,1},{2,18},{18,2},{3,19},{19,3},{4,20},{20... | collective-permute-start | bytes 20 | tf_op jit(solution)/shard_map/ppermute | solution.py:585
  16.8 228.3 %conditional.1 = (f32[3,512]{1,0:T(4,128)S(1)}) conditional(s32[]{:T(128)} %clamp.3, (s32[512]{0:T(512)S(1)}, s32[512,4]{0,1:T(4,128)S(1)}, bf16[384]{0:T(512)(128)(2,1)}, bf16[512,384]{1,0:T(8,128)(2,1)}, bf16[384]{0:T(512)(128)(2,1)}, /*index=5*/bf16[6144,2048]{1,0:T(8,128)(2,1)}, bf16[6144,2048]{1,0:T(8,128)(2,1)}, ...), branch_computations={%region_7.15_spmd, %region_15.23_spmd, %region_23.31_spmd, %region... | conditional | flops 41886638080 | bytes 307196608 | solution.py:595
  27.6 2.6 branch_2_fun.12
  33.3 2.2 collective-permute-start.91
  35.6 5.8 %collective-permute-done.90 = bf16[256,384]{1,0:T(8,128)(2,1)S(1)} collective-permute-done((bf16[256,384]{1,0:T(8,128)(2,1)}, bf16[256,384]{1,0:T(8,128)(2,1)S(1)}, u32[]{:S(2)}, u32[]{:S(2)}) %collective-permute-start.90) | collective-permute-done | bytes 196640 | tf_op jit(solution)/shard_map/cond/branch_2_fun/ppermute | solution.py:129
  41.4 3.3 %collective-permute-done.91 = bf16[256,384]{1,0:T(8,128)(2,1)S(1)} collective-permute-done((bf16[256,384]{1,0:T(8,128)(2,1)}, bf16[256,384]{1,0:T(8,128)(2,1)S(1)}, u32[]{:S(2)}, u32[]{:S(2)}) %collective-permute-start.91) | collective-permute-done | bytes 196640 | tf_op jit(solution)/shard_map/cond/branch_2_fun/ppermute | solution.py:129
  46.3 9.0 %collective-permute-done.97.refs_1_ = bf16[512,384]{1,0:T(8,128)(2,1)S(1)} collective-permute-done((bf16[512,384]{1,0:T(8,128)(2,1)S(1)}, bf16[512,384]{1,0:T(8,128)(2,1)S(1)}, u32[]{:S(2)}, u32[]{:S(2)}) %collective-permute-start.97) | collective-permute-done | bytes 393248 | tf_op jit(solution)/shard_map/cond/branch_2_fun/ppermute | solution.py:129
  64.0 9.3 %branch_2_fun.13 = (f32[256,2048]{1,0:T(8,128)}, f32[256,2048]{1,0:T(8,128)}) custom-call(s32[5]{0:T(128)} %stack.230.where_ref, bf16[256,384]{1,0:T(8,128)(2,1)} %get-tuple-element.229.refs_0_, bf16[256,384]{1,0:T(8,128)(2,1)} %copy-done.119, bf16[256,384]{1,0:T(8,128)(2,1)} %copy-done.120, bf16[256,384]{1,0:T(8,128)(2,1)} %copy-done.121, ...), custom_call_target="tpu_custom_call" | custom-call | flops 3221225472 | bytes 20971520 | tf_op jit(solution)/shard_map/cond/branch_2_fun/pallas_call | solution.py:274
  77.8 16.3 %branch_2_fun.14 = (f32[256,2048]{1,0:T(8,128)}, f32[256,2048]{1,0:T(8,128)}) custom-call(s32[6]{0:T(128)} %stack.233.where_ref, bf16[512,384]{1,0:T(8,128)(2,1)} %copy-done.6, bf16[512,384]{1,0:T(8,128)(2,1)} %copy-done.43, bf16[512,384]{1,0:T(8,128)(2,1)} %copy-done.44, ...), custom_call_target="tpu_custom_call", output_to_operand_aliasing={{0}: (9, {}), {1}: (10, {})} | custom-call | flops 6442450944 | bytes 33554432 | tf_op jit(solution)/shard_map/cond/branch_2_fun/pallas_call | solution.py:274
  97.4 10.2 %branch_2_fun.15.h_ref = bf16[256,2048]{1,0:T(8,128)(2,1)} custom-call(s32[5]{0:T(128)} %stack.227.where_ref, bf16[256,384]{1,0:T(8,128)(2,1)} %copy-done.132, bf16[256,384]{1,0:T(8,128)(2,1)} %copy-done.133, bf16[256,384]{1,0:T(8,128)(2,1)} %copy-done.134, bf16[256,384]{1,0:T(8,128)(2,1)} %copy-done.135, ...), custom_call_target="tpu_custom_call" | custom-call | flops 3221225472 | bytes 20971520 | tf_op jit(solution)/shard_map/cond/branch_2_fun/pallas_call | solution.py:274
  107.6 6.3 %branch_2_fun.16 = (f32[256,384]{1,0:T(8,128)}, f32[256,384]{1,0:T(8,128)}, bf16[512,384]{1,0:T(8,128)(2,1)}) custom-call(s32[5]{0:T(128)} %stack.227.where_ref, bf16[256,2048]{1,0:T(8,128)(2,1)} %branch_2_fun.15.h_ref, bf16[2048,6144]{1,0:T(8,128)(2,1)} %get-tuple-element.239.w_ref, f32[256,1]{1,0:T(8,128)} %copy.190.gate_ref), custom_call_target="tpu_custom_call" | custom-call | flops 1610612736 | bytes 8650752 | tf_op jit(solution)/shard_map/cond/branch_2_fun/pallas_call | solution.py:313
  115.8 6.1 %branch_2_fun.17 = (f32[256,384]{1,0:T(8,128)}, f32[256,384]{1,0:T(8,128)}, bf16[512,384]{1,0:T(8,128)(2,1)}) custom-call(s32[5]{0:T(128)} %stack.235.where_ref, bf16[256,2048]{1,0:T(8,128)(2,1)} %branch_2_fun.15.h_ref, bf16[2048,6144]{1,0:T(8,128)(2,1)} %get-tuple-element.239.w_ref, f32[256,1]{1,0:T(8,128)} %copy.190.gate_ref), custom_call_target="tpu_custom_call" | custom-call | flops 1610612736 | bytes 8650752 | tf_op jit(solution)/shard_map/cond/branch_2_fun/pallas_call | solution.py:313
  121.9 6.3 %branch_2_fun.18 = (f32[256,384]{1,0:T(8,128)}, f32[256,384]{1,0:T(8,128)}, bf16[512,384]{1,0:T(8,128)(2,1)}) custom-call(s32[5]{0:T(128)} %stack.234.where_ref, bf16[256,2048]{1,0:T(8,128)(2,1)} %branch_2_fun.15.h_ref, bf16[2048,6144]{1,0:T(8,128)(2,1)} %get-tuple-element.239.w_ref, f32[256,1]{1,0:T(8,128)} %copy.190.gate_ref), custom_call_target="tpu_custom_call" | custom-call | flops 1610612736 | bytes 8650752 | tf_op jit(solution)/shard_map/cond/branch_2_fun/pallas_call | solution.py:313
  130.9 5.6 %collective-permute-done.109 = bf16[256,384]{1,0:T(8,128)(2,1)S(1)} collective-permute-done((bf16[256,384]{1,0:T(8,128)(2,1)S(1)}, bf16[256,384]{1,0:T(8,128)(2,1)S(1)}, u32[]{:S(2)}, u32[]{:S(2)}) %collective-permute-start.109) | collective-permute-done | bytes 196640 | tf_op jit(solution)/shard_map/cond/branch_2_fun/ppermute | solution.py:129
  136.7 6.3 %branch_2_fun.19 = (f32[256,384]{1,0:T(8,128)}, f32[256,384]{1,0:T(8,128)}, bf16[512,384]{1,0:T(8,128)(2,1)}) custom-call(s32[5]{0:T(128)} %stack.230.where_ref, bf16[256,2048]{1,0:T(8,128)(2,1)} %branch_2_fun.15.h_ref, bf16[2048,6144]{1,0:T(8,128)(2,1)} %get-tuple-element.239.w_ref, f32[256,1]{1,0:T(8,128)} %copy.190.gate_ref), custom_call_target="tpu_custom_call" | custom-call | flops 1610612736 | bytes 8650752 | tf_op jit(solution)/shard_map/cond/branch_2_fun/pallas_call | solution.py:313
  147.3 4.6 %collective-permute-done.116 = bf16[256,384]{1,0:T(8,128)(2,1)S(1)} collective-permute-done((bf16[256,384]{1,0:T(8,128)(2,1)S(1)}, bf16[256,384]{1,0:T(8,128)(2,1)S(1)}, u32[]{:S(2)}, u32[]{:S(2)}) %collective-permute-start.116) | collective-permute-done | bytes 196640 | tf_op jit(solution)/shard_map/cond/branch_2_fun/ppermute | solution.py:129
  152.0 3.2 %collective-permute-start.117 = (bf16[256,384]{1,0:T(8,128)(2,1)S(1)}, bf16[256,384]{1,0:T(8,128)(2,1)S(1)}, u32[]{:S(2)}, u32[]{:S(2)}) collective-permute-start(bf16[256,384]{1,0:T(8,128)(2,1)S(1)} %add_convert_fusion.16), channel_id=1, source_target_pairs={{0,12},{1,13},{2,14},{3,15},{4,0},{5,1},{6,2},{7,3},{8,4},{9,5},{1... | collective-permute-start | bytes 589832 | tf_op jit(solution)/shard_map/cond/branch_2_fun/ppermute | solution.py:129
  156.1 2.3 collective-permute-done.117.e3
  159.2 2.7 %branch_2_fun.20 = (bf16[320,384]{1,0:T(8,128)(2,1)}, f32[320,1]{1,0:T(8,128)}) custom-call(s32[320,4]{1,0:T(8,128)} %copy.194.slot_ref, bf16[320,384]{1,0:T(8,128)(2,1)} %get-tuple-element.223.x_ref, bf16[1,384]{1,0:T(2,128)(2,1)} %broadcast_in_dim.531.gain_ref, bf16[256,384]{1,0:T(8,128)(2,1)} %add_convert_fusion.21.e0, bf16[256,384]{1,0:T(8,128)(2,1)} %copy-done.130, ...), custom_call_target="tpu_custom_call" | custom-call | tf_op jit(solution)/shard_map/cond/branch_2_fun/pallas_call | solution.py:352
  163.8 2.2 collective-permute-start.119
  166.0 6.6 %collective-permute-done.118 = bf16[320,384]{1,0:T(8,128)(2,1)S(1)} collective-permute-done((bf16[320,384]{1,0:T(8,128)(2,1)}, bf16[320,384]{1,0:T(8,128)(2,1)S(1)}, u32[]{:S(2)}, u32[]{:S(2)}) %collective-permute-start.118) | collective-permute-done | bytes 245792 | tf_op jit(solution)/shard_map/cond/branch_2_fun/ppermute | solution.py:129
  172.7 2.1 collective-permute-done.119
  176.9 12.1 %collective-permute-done.125.refs_1_ = bf16[640,384]{1,0:T(8,128)(2,1)S(1)} collective-permute-done((bf16[640,384]{1,0:T(8,128)(2,1)S(1)}, bf16[640,384]{1,0:T(8,128)(2,1)S(1)}, u32[]{:S(2)}, u32[]{:S(2)}) %collective-permute-start.125) | collective-permute-done | bytes 491552 | tf_op jit(solution)/shard_map/cond/branch_2_fun/ppermute | solution.py:129
  189.5 3.0 %collective-permute-done.121.refs_1_ = bf16[320,384]{1,0:T(8,128)(2,1)S(1)} collective-permute-done((bf16[320,384]{1,0:T(8,128)(2,1)}, bf16[320,384]{1,0:T(8,128)(2,1)S(1)}, u32[]{:S(2)}, u32[]{:S(2)}) %collective-permute-start.121) | collective-permute-done | bytes 245792 | tf_op jit(solution)/shard_map/cond/branch_2_fun/ppermute | solution.py:129
  195.5 3.1 %collective-permute-done.131 = f32[320]{0:T(512)S(1)} collective-permute-done((f32[320]{0:T(512)S(1)}, f32[320]{0:T(512)S(1)}, u32[]{:S(2)}, u32[]{:S(2)}) %collective-permute-start.131) | collective-permute-done | bytes 1312 | tf_op jit(solution)/shard_map/cond/branch_2_fun/ppermute | solution.py:129
  199.6 2.9 %collective-permute-start.133 = (f32[320]{0:T(512)S(1)}, f32[320]{0:T(512)S(1)}, u32[]{:S(2)}, u32[]{:S(2)}) collective-permute-start(f32[320]{0:T(512)S(1)} %add.548), channel_id=1, source_target_pairs={{0,8},{1,9},{2,10},{3,11},{4,12},{5,13},{6,14},{7,15},{8,0},{9,1},... | collective-permute-start | bytes 3848 | tf_op jit(solution)/shard_map/cond/branch_2_fun/ppermute | solution.py:129
  202.5 7.2 %branch_2_fun.21.refs_6_ = f32[320,2048]{1,0:T(8,128)} custom-call(s32[5]{0:T(128)} %stack.230.where_ref, bf16[320,384]{1,0:T(8,128)(2,1)} %get-tuple-element.257.refs_0_, bf16[320,384]{1,0:T(8,128)(2,1)} %copy-done.99, bf16[320,384]{1,0:T(8,128)(2,1)} %copy-done.100, bf16[320,384]{1,0:T(8,128)(2,1)} %copy-done.101, ...), custom_call_target="tpu_custom_call" | custom-call | flops 2013265920 | bytes 11534336 | tf_op jit(solution)/shard_map/cond/branch_2_fun/pallas_call | solution.py:434
  209.7 2.4 collective-permute-done.120.refs_0_
  213.9 11.2 %branch_2_fun.22.refs_5_ = f32[320,2048]{1,0:T(8,128)} custom-call(s32[6]{0:T(128)} %stack.233.where_ref, bf16[640,384]{1,0:T(8,128)(2,1)} %copy-done.3, bf16[640,384]{1,0:T(8,128)(2,1)} %copy-done.27, bf16[640,384]{1,0:T(8,128)(2,1)} %copy-done.28, bf16[640,384]{1,0:T(8,128)(2,1)} %copy-done.29, ...), custom_call_target="tpu_custom_call", output_to_operand_aliasing={{}: (7, {})} | custom-call | flops 4026531840 | bytes 17825792 | tf_op jit(solution)/shard_map/cond/branch_2_fun/pallas_call | solution.py:434
  228.2 8.4 %branch_2_fun.23 = f32[320,128]{1,0:T(8,128)} custom-call(s32[5]{0:T(128)} %stack.227.where_ref, bf16[320,384]{1,0:T(8,128)(2,1)} %copy-done.95, bf16[320,384]{1,0:T(8,128)(2,1)} %copy-done.96, bf16[320,384]{1,0:T(8,128)(2,1)} %copy-done.97, bf16[320,384]{1,0:T(8,128)(2,1)} %copy-done.98, bf16[6144,2048]{1,0:T(8,128)(2,1)} %get-tuple-element.258.refs_4_.refs_5_, ...), custom_call_target="tpu_custom_call" | custom-call | flops 2013265920 | bytes 11534336 | tf_op jit(solution)/shard_map/cond/branch_2_fun/pallas_call | solution.py:434
  245.8 3.9 %all-to-all-start = ((f32[16,3,32]{2,1,0:T(4,128)}), f32[16,3,32]{2,1,0:T(4,128)S(1)}, u32[]{:S(2)}, u32[]{:S(2)}) async-start(f32[16,3,32]{2,1,0:T(4,128)} %copy.213), calls=%async_computation | async-start | bytes 65536 | tf_op jit(solution)/shard_map/all_to_all | solution.py:616
  249.8 6.6 %all-to-all-done = f32[16,3,32]{2,1,0:T(4,128)S(1)} async-done(((f32[16,3,32]{2,1,0:T(4,128)}), f32[16,3,32]{2,1,0:T(4,128)S(1)}, u32[]{:S(2)}, u32[]{:S(2)}) %all-to-all-start) | async-done | bytes 6176 | tf_op jit(solution)/shard_map/all_to_all | solution.py:616
  (211 shorter events, 57.2 us)
Async XLA Ops:
  30.2 15.7 %collective-permute-start.93 = (bf16[256,384]{1,0:T(8,128)(2,1)}, bf16[256,384]{1,0:T(8,128)(2,1)S(1)}, u32[]{:S(2)}, u32[]{:S(2)}) collective-permute-start(bf16[256,384]{1,0:T(8,128)(2,1)} %get-tuple-element.229.refs_0_), channel_id=1, source_target_pairs={{0,2},{1,3},{2,0},{3,1},{4,6},{5,7},{6,4},{7,5},{8,10},{9,11},{10,... | collective-permute-start | bytes 589832 | tf_op jit(solution)/shard_map/cond/branch_2_fun/ppermute | solution.py:129
  31.7 29.3 %collective-permute-start.94 = (bf16[256,384]{1,0:T(8,128)(2,1)}, bf16[256,384]{1,0:T(8,128)(2,1)S(1)}, u32[]{:S(2)}, u32[]{:S(2)}) collective-permute-start(bf16[256,384]{1,0:T(8,128)(2,1)} %get-tuple-element.229.refs_0_), channel_id=1, source_target_pairs={{0,1},{1,0},{2,3},{3,2},{4,5},{5,4},{6,7},{7,6},{8,9},{9,8},{10,11... | collective-permute-start | bytes 589832 | tf_op jit(solution)/shard_map/cond/branch_2_fun/ppermute | solution.py:129
  31.7 9.7 %collective-permute-start.90 = (bf16[256,384]{1,0:T(8,128)(2,1)}, bf16[256,384]{1,0:T(8,128)(2,1)S(1)}, u32[]{:S(2)}, u32[]{:S(2)}) collective-permute-start(bf16[256,384]{1,0:T(8,128)(2,1)} %get-tuple-element.226), channel_id=1, source_target_pairs={{0,4},{1,5},{2,6},{3,7},{4,8},{5,9},{6,10},{7,11},{8,12},{9,13},{1... | collective-permute-start | bytes 589832 | tf_op jit(solution)/shard_map/cond/branch_2_fun/ppermute | solution.py:129
  33.3 11.5 %collective-permute-start.91 = (bf16[256,384]{1,0:T(8,128)(2,1)}, bf16[256,384]{1,0:T(8,128)(2,1)S(1)}, u32[]{:S(2)}, u32[]{:S(2)}) collective-permute-start(bf16[256,384]{1,0:T(8,128)(2,1)} %get-tuple-element.227), channel_id=1, source_target_pairs={{0,12},{1,13},{2,14},{3,15},{4,0},{5,1},{6,2},{7,3},{8,4},{9,5},{1... | collective-permute-start | bytes 589832 | tf_op jit(solution)/shard_map/cond/branch_2_fun/ppermute | solution.py:129
  35.5 19.9 %collective-permute-start.102 = (f32[512]{0:T(512)S(1)}, f32[512]{0:T(512)S(1)}, u32[]{:S(2)}, u32[]{:S(2)}) collective-permute-start(f32[512]{0:T(512)S(1)} %get-tuple-element.238), channel_id=1, source_target_pairs={{0,1},{1,0},{2,3},{3,2},{4,5},{5,4},{6,7},{7,6},{8,9},{9,8},{10,11... | collective-permute-start | bytes 6152 | tf_op jit(solution)/shard_map/cond/branch_2_fun/ppermute | solution.py:129
  44.8 10.6 %collective-permute-start.97 = (bf16[512,384]{1,0:T(8,128)(2,1)S(1)}, bf16[512,384]{1,0:T(8,128)(2,1)S(1)}, u32[]{:S(2)}, u32[]{:S(2)}) collective-permute-start(bf16[512,384]{1,0:T(8,128)(2,1)S(1)} %constant_dynamic-update-slice_fusion.8.refs_0_), channel_id=1, source_target_pairs={{0,2},{1,3},{2,0},{3,1},{4,6},{5,7},{6,4},{7,5},{8,10},{9,11},{10,... | collective-permute-start | bytes 1179656 | tf_op jit(solution)/shard_map/cond/branch_2_fun/ppermute | solution.py:129
  45.8 29.8 %collective-permute-start.98 = (bf16[512,384]{1,0:T(8,128)(2,1)S(1)}, bf16[512,384]{1,0:T(8,128)(2,1)S(1)}, u32[]{:S(2)}, u32[]{:S(2)}) collective-permute-start(bf16[512,384]{1,0:T(8,128)(2,1)S(1)} %constant_dynamic-update-slice_fusion.8.refs_0_), channel_id=1, source_target_pairs={{0,1},{1,0},{2,3},{3,2},{4,5},{5,4},{6,7},{7,6},{8,9},{9,8},{10,11... | collective-permute-start | bytes 1179656 | tf_op jit(solution)/shard_map/cond/branch_2_fun/ppermute | solution.py:129
  45.9 16.4 %collective-permute-start.95 = (bf16[256,384]{1,0:T(8,128)(2,1)S(1)}, bf16[256,384]{1,0:T(8,128)(2,1)S(1)}, u32[]{:S(2)}, u32[]{:S(2)}) collective-permute-start(bf16[256,384]{1,0:T(8,128)(2,1)S(1)} %collective-permute-done.93.refs_1_), channel_id=1, source_target_pairs={{0,1},{1,0},{2,3},{3,2},{4,5},{5,4},{6,7},{7,6},{8,9},{9,8},{10,11... | collective-permute-start | bytes 589832 | tf_op jit(solution)/shard_map/cond/branch_2_fun/ppermute | solution.py:129
  55.3 21.7 %collective-permute-start.99 = (bf16[512,384]{1,0:T(8,128)(2,1)S(1)}, bf16[512,384]{1,0:T(8,128)(2,1)S(1)}, u32[]{:S(2)}, u32[]{:S(2)}) collective-permute-start(bf16[512,384]{1,0:T(8,128)(2,1)S(1)} %collective-permute-done.97.refs_1_), channel_id=1, source_target_pairs={{0,1},{1,0},{2,3},{3,2},{4,5},{5,4},{6,7},{7,6},{8,9},{9,8},{10,11... | collective-permute-start | bytes 1179656 | tf_op jit(solution)/shard_map/cond/branch_2_fun/ppermute | solution.py:129
  59.3 34.9 %collective-permute-start.104 = (f32[512]{0:T(512)S(1)}, f32[512]{0:T(512)S(1)}, u32[]{:S(2)}, u32[]{:S(2)}) collective-permute-start(f32[512]{0:T(512)S(1)} %add.530), channel_id=1, source_target_pairs={{0,4},{1,5},{2,6},{3,7},{4,8},{5,9},{6,10},{7,11},{8,12},{9,13},{1... | collective-permute-start | bytes 6152 | tf_op jit(solution)/shard_map/cond/branch_2_fun/ppermute | solution.py:129
  61.0 33.2 %collective-permute-start.105 = (f32[512]{0:T(512)S(1)}, f32[512]{0:T(512)S(1)}, u32[]{:S(2)}, u32[]{:S(2)}) collective-permute-start(f32[512]{0:T(512)S(1)} %add.530), channel_id=1, source_target_pairs={{0,8},{1,9},{2,10},{3,11},{4,12},{5,13},{6,14},{7,15},{8,0},{9,1},... | collective-permute-start | bytes 6152 | tf_op jit(solution)/shard_map/cond/branch_2_fun/ppermute | solution.py:129
  62.3 11.7 %collective-permute-start.92 = (bf16[256,384]{1,0:T(8,128)(2,1)}, bf16[256,384]{1,0:T(8,128)(2,1)S(1)}, u32[]{:S(2)}, u32[]{:S(2)}) collective-permute-start(bf16[256,384]{1,0:T(8,128)(2,1)} %get-tuple-element.228), channel_id=1, source_target_pairs={{0,8},{1,9},{2,10},{3,11},{4,12},{5,13},{6,14},{7,15},{8,0},{9,1},... | collective-permute-start | bytes 589832 | tf_op jit(solution)/shard_map/cond/branch_2_fun/ppermute | solution.py:129
  74.0 20.2 %collective-permute-start.106 = (f32[512]{0:T(512)S(1)}, f32[512]{0:T(512)S(1)}, u32[]{:S(2)}, u32[]{:S(2)}) collective-permute-start(f32[512]{0:T(512)S(1)} %add.530), channel_id=1, source_target_pairs={{0,12},{1,13},{2,14},{3,15},{4,0},{5,1},{6,2},{7,3},{8,4},{9,5},{1... | collective-permute-start | bytes 6152 | tf_op jit(solution)/shard_map/cond/branch_2_fun/ppermute | solution.py:129
  75.5 18.5 %collective-permute-start.96 = (bf16[256,384]{1,0:T(8,128)(2,1)S(1)}, bf16[256,384]{1,0:T(8,128)(2,1)S(1)}, u32[]{:S(2)}, u32[]{:S(2)}) collective-permute-start(bf16[256,384]{1,0:T(8,128)(2,1)S(1)} %collective-permute-done.92.refs_0_), channel_id=1, source_target_pairs={{0,2},{1,3},{2,0},{3,1},{4,6},{5,7},{6,4},{7,5},{8,10},{9,11},{10,... | collective-permute-start | bytes 589832 | tf_op jit(solution)/shard_map/cond/branch_2_fun/ppermute | solution.py:129
  77.0 19.0 %collective-permute-start.100 = (bf16[256,384]{1,0:T(8,128)(2,1)S(1)}, bf16[256,384]{1,0:T(8,128)(2,1)S(1)}, u32[]{:S(2)}, u32[]{:S(2)}) collective-permute-start(bf16[256,384]{1,0:T(8,128)(2,1)S(1)} %collective-permute-done.92.refs_0_), channel_id=1, source_target_pairs={{0,1},{1,0},{2,3},{3,2},{4,5},{5,4},{6,7},{7,6},{8,9},{9,8},{10,11... | collective-permute-start | bytes 589832 | tf_op jit(solution)/shard_map/cond/branch_2_fun/ppermute | solution.py:129
  128.2 15.8 %collective-permute-start.115 = (bf16[512,384]{1,0:T(8,128)(2,1)}, bf16[512,384]{1,0:T(8,128)(2,1)S(1)}, u32[]{:S(2)}, u32[]{:S(2)}) collective-permute-start(bf16[512,384]{1,0:T(8,128)(2,1)} %get-tuple-element.254), channel_id=1, source_target_pairs={{0,1},{1,0},{2,3},{3,2},{4,5},{5,4},{6,7},{7,6},{8,9},{9,8},{10,11... | collective-permute-start | bytes 1179656 | tf_op jit(solution)/shard_map/cond/branch_2_fun/ppermute | solution.py:129
  129.4 13.7 %collective-permute-start.112 = (bf16[256,384]{1,0:T(8,128)(2,1)S(1)}, bf16[256,384]{1,0:T(8,128)(2,1)S(1)}, u32[]{:S(2)}, u32[]{:S(2)}) collective-permute-start(bf16[256,384]{1,0:T(8,128)(2,1)S(1)} %add_convert_fusion.20), channel_id=1, source_target_pairs={{0,2},{1,3},{2,0},{3,1},{4,6},{5,7},{6,4},{7,5},{8,10},{9,11},{10,... | collective-permute-start | bytes 589832 | tf_op jit(solution)/shard_map/cond/branch_2_fun/ppermute | solution.py:129
  136.6 19.5 %collective-permute-start.114 = (bf16[256,384]{1,0:T(8,128)(2,1)S(1)}, bf16[256,384]{1,0:T(8,128)(2,1)S(1)}, u32[]{:S(2)}, u32[]{:S(2)}) collective-permute-start(bf16[256,384]{1,0:T(8,128)(2,1)S(1)} %add_convert_fusion.18), channel_id=1, source_target_pairs={{0,8},{1,9},{2,10},{3,11},{4,12},{5,13},{6,14},{7,15},{8,0},{9,1},... | collective-permute-start | bytes 589832 | tf_op jit(solution)/shard_map/cond/branch_2_fun/ppermute | solution.py:129
  143.1 13.0 %collective-permute-start.113 = (bf16[256,384]{1,0:T(8,128)(2,1)S(1)}, bf16[256,384]{1,0:T(8,128)(2,1)S(1)}, u32[]{:S(2)}, u32[]{:S(2)}) collective-permute-start(bf16[256,384]{1,0:T(8,128)(2,1)S(1)} %add_convert_fusion.19), channel_id=1, source_target_pairs={{0,4},{1,5},{2,6},{3,7},{4,8},{5,9},{6,10},{7,11},{8,12},{9,13},{1... | collective-permute-start | bytes 589832 | tf_op jit(solution)/shard_map/cond/branch_2_fun/ppermute | solution.py:129
  161.9 10.8 %collective-permute-start.118 = (bf16[320,384]{1,0:T(8,128)(2,1)}, bf16[320,384]{1,0:T(8,128)(2,1)S(1)}, u32[]{:S(2)}, u32[]{:S(2)}) collective-permute-start(bf16[320,384]{1,0:T(8,128)(2,1)} %get-tuple-element.257.refs_0_), channel_id=1, source_target_pairs={{0,4},{1,5},{2,6},{3,7},{4,8},{5,9},{6,10},{7,11},{8,12},{9,13},{1... | collective-permute-start | bytes 737288 | tf_op jit(solution)/shard_map/cond/branch_2_fun/ppermute | solution.py:129
  163.8 10.9 %collective-permute-start.119 = (bf16[320,384]{1,0:T(8,128)(2,1)}, bf16[320,384]{1,0:T(8,128)(2,1)S(1)}, u32[]{:S(2)}, u32[]{:S(2)}) collective-permute-start(bf16[320,384]{1,0:T(8,128)(2,1)} %get-tuple-element.257.refs_0_), channel_id=1, source_target_pairs={{0,12},{1,13},{2,14},{3,15},{4,0},{5,1},{6,2},{7,3},{8,4},{9,5},{1... | collective-permute-start | bytes 737288 | tf_op jit(solution)/shard_map/cond/branch_2_fun/ppermute | solution.py:129
  174.8 14.2 %collective-permute-start.125 = (bf16[640,384]{1,0:T(8,128)(2,1)S(1)}, bf16[640,384]{1,0:T(8,128)(2,1)S(1)}, u32[]{:S(2)}, u32[]{:S(2)}) collective-permute-start(bf16[640,384]{1,0:T(8,128)(2,1)S(1)} %constant_dynamic-update-slice_fusion.10.refs_0_), channel_id=1, source_target_pairs={{0,2},{1,3},{2,0},{3,1},{4,6},{5,7},{6,4},{7,5},{8,10},{9,11},{10,... | collective-permute-start | bytes 1474568 | tf_op jit(solution)/shard_map/cond/branch_2_fun/ppermute | solution.py:129
  175.3 17.2 %collective-permute-start.121 = (bf16[320,384]{1,0:T(8,128)(2,1)}, bf16[320,384]{1,0:T(8,128)(2,1)S(1)}, u32[]{:S(2)}, u32[]{:S(2)}) collective-permute-start(bf16[320,384]{1,0:T(8,128)(2,1)} %get-tuple-element.257.refs_0_), channel_id=1, source_target_pairs={{0,2},{1,3},{2,0},{3,1},{4,6},{5,7},{6,4},{7,5},{8,10},{9,11},{10,... | collective-permute-start | bytes 737288 | tf_op jit(solution)/shard_map/cond/branch_2_fun/ppermute | solution.py:129
  176.9 35.7 %collective-permute-start.126 = (bf16[640,384]{1,0:T(8,128)(2,1)S(1)}, bf16[640,384]{1,0:T(8,128)(2,1)S(1)}, u32[]{:S(2)}, u32[]{:S(2)}) collective-permute-start(bf16[640,384]{1,0:T(8,128)(2,1)S(1)} %constant_dynamic-update-slice_fusion.10.refs_0_), channel_id=1, source_target_pairs={{0,1},{1,0},{2,3},{3,2},{4,5},{5,4},{6,7},{7,6},{8,9},{9,8},{10,11... | collective-permute-start | bytes 1474568 | tf_op jit(solution)/shard_map/cond/branch_2_fun/ppermute | solution.py:129
  189.0 24.1 %collective-permute-start.127 = (bf16[640,384]{1,0:T(8,128)(2,1)S(1)}, bf16[640,384]{1,0:T(8,128)(2,1)S(1)}, u32[]{:S(2)}, u32[]{:S(2)}) collective-permute-start(bf16[640,384]{1,0:T(8,128)(2,1)S(1)} %collective-permute-done.125.refs_1_), channel_id=1, source_target_pairs={{0,1},{1,0},{2,3},{3,2},{4,5},{5,4},{6,7},{7,6},{8,9},{9,8},{10,11... | collective-permute-start | bytes 1474568 | tf_op jit(solution)/shard_map/cond/branch_2_fun/ppermute | solution.py:129
  198.6 13.5 %collective-permute-start.120 = (bf16[320,384]{1,0:T(8,128)(2,1)}, bf16[320,384]{1,0:T(8,128)(2,1)S(1)}, u32[]{:S(2)}, u32[]{:S(2)}) collective-permute-start(bf16[320,384]{1,0:T(8,128)(2,1)} %get-tuple-element.257.refs_0_), channel_id=1, source_target_pairs={{0,8},{1,9},{2,10},{3,11},{4,12},{5,13},{6,14},{7,15},{8,0},{9,1},... | collective-permute-start | bytes 737288 | tf_op jit(solution)/shard_map/cond/branch_2_fun/ppermute | solution.py:129
  198.8 27.2 %collective-permute-start.132 = (f32[320]{0:T(512)S(1)}, f32[320]{0:T(512)S(1)}, u32[]{:S(2)}, u32[]{:S(2)}) collective-permute-start(f32[320]{0:T(512)S(1)} %add.548), channel_id=1, source_target_pairs={{0,4},{1,5},{2,6},{3,7},{4,8},{5,9},{6,10},{7,11},{8,12},{9,13},{1... | collective-permute-start | bytes 3848 | tf_op jit(solution)/shard_map/cond/branch_2_fun/ppermute | solution.py:129
  199.6 26.4 %collective-permute-start.133 = (f32[320]{0:T(512)S(1)}, f32[320]{0:T(512)S(1)}, u32[]{:S(2)}, u32[]{:S(2)}) collective-permute-start(f32[320]{0:T(512)S(1)} %add.548), channel_id=1, source_target_pairs={{0,8},{1,9},{2,10},{3,11},{4,12},{5,13},{6,14},{7,15},{8,0},{9,1},... | collective-permute-start | bytes 3848 | tf_op jit(solution)/shard_map/cond/branch_2_fun/ppermute | solution.py:129
  212.1 13.9 %collective-permute-start.134 = (f32[320]{0:T(512)S(1)}, f32[320]{0:T(512)S(1)}, u32[]{:S(2)}, u32[]{:S(2)}) collective-permute-start(f32[320]{0:T(512)S(1)} %add.548), channel_id=1, source_target_pairs={{0,12},{1,13},{2,14},{3,15},{4,0},{5,1},{6,2},{7,3},{8,4},{9,5},{1... | collective-permute-start | bytes 3848 | tf_op jit(solution)/shard_map/cond/branch_2_fun/ppermute | solution.py:129
  212.6 12.5 %collective-permute-start.124 = (bf16[320,384]{1,0:T(8,128)(2,1)S(1)}, bf16[320,384]{1,0:T(8,128)(2,1)S(1)}, u32[]{:S(2)}, u32[]{:S(2)}) collective-permute-start(bf16[320,384]{1,0:T(8,128)(2,1)S(1)} %collective-permute-done.120.refs_0_), channel_id=1, source_target_pairs={{0,2},{1,3},{2,0},{3,1},{4,6},{5,7},{6,4},{7,5},{8,10},{9,11},{10,... | collective-permute-start | bytes 737288 | tf_op jit(solution)/shard_map/cond/branch_2_fun/ppermute | solution.py:129
  213.1 13.7 %collective-permute-start.128 = (bf16[320,384]{1,0:T(8,128)(2,1)S(1)}, bf16[320,384]{1,0:T(8,128)(2,1)S(1)}, u32[]{:S(2)}, u32[]{:S(2)}) collective-permute-start(bf16[320,384]{1,0:T(8,128)(2,1)S(1)} %collective-permute-done.120.refs_0_), channel_id=1, source_target_pairs={{0,1},{1,0},{2,3},{3,2},{4,5},{5,4},{6,7},{7,6},{8,9},{9,8},{10,11... | collective-permute-start | bytes 737288 | tf_op jit(solution)/shard_map/cond/branch_2_fun/ppermute | solution.py:129
  245.8 10.6 %all-to-all-start = ((f32[16,3,32]{2,1,0:T(4,128)}), f32[16,3,32]{2,1,0:T(4,128)S(1)}, u32[]{:S(2)}, u32[]{:S(2)}) async-start(f32[16,3,32]{2,1,0:T(4,128)} %copy.213), calls=%async_computation | async-start | bytes 65536 | tf_op jit(solution)/shard_map/all_to_all | solution.py:616
  (49 other events, 399.7 us)
